TPU v7x, 128 devices: a whole 4x4x4 slice. The times are simulated.
128 devices in a mesh: gx: 8 (over z, core), gy: 16 (over y, x).
Axes of the slice: x: 4, y: 4, z: 4, core: 2. Of those that a mesh axis runs over, the one named last changes fastest.
Arguments:
- offsets: float32 [3, 2097152], P(None, ('gx', 'gy')), may hold values from -5 to 5
- weights: float32 [2097152], P(('gx', 'gy')), may hold values from -1 to 1
- owners: int32 [16384, 1], P(('gx', 'gy')), may hold values from 0 to 127; in each aligned block of 128 rows (0 to 127, 128 to 255, ...) at most 2 rows name the same one
- cells: int32 [2097152], P(('gx', 'gy')), may hold values from 0 to 65535
Outputs:
- spectrum: float32 [2, 6, 64, 1024, 128], P(None, None, 'gx', 'gy')
Inputs may be any that keep to these rules, and one draw needn't show every extreme that they name: owners numbers devices as gx index times the size of gy plus gy index; among the 128 blocks of one device at most 2 have the same owner, and some device has exactly 2 blocks for one owner. cells numbers the cells of the owner's block as (x * 64 + y) * 128 + z.
All inputs are finite; a program needn't handle non-finite values.
Results may differ from a plain program's by a relative error of at most 0.0029.
Values may be sent and summed in bfloat16 or wider, within the bound.
A program may use at most 128 MiB of HBM per device.

v0:
```python
import math

import jax
import jax.numpy as jnp
from jax import lax
from jax.sharding import PartitionSpec as P

CX = 8
CY = 64
NZ = 128
CAP = 2


def swapped(value, axis, apart):
    return lax.ppermute(value, axis, [(i, i ^ 1 << apart) for i in range(lax.axis_size(axis))])


def quad_terms(offsets, weights):
    along_x = offsets[0]
    along_y = offsets[1]
    along_z = offsets[2]
    scaled = weights / jnp.maximum(along_x * along_x + along_y * along_y + along_z * along_z, 0.25)
    return jnp.stack(
        [
            along_x * along_x * scaled,
            along_y * along_y * scaled,
            along_z * along_z * scaled,
            along_x * along_y * scaled,
            along_y * along_z * scaled,
            along_z * along_x * scaled,
        ]
    ).astype(jnp.bfloat16)


def flip_bits(value, width):
    result = 0
    for position_bit in range(width):
        result = result + (value >> position_bit & 1) * (1 << width - 1 - position_bit)
    return result


def rotation(first_index, second_index, length):
    phase_int = first_index[:, None] * second_index[None, :] % length
    angle_rad = phase_int.astype(jnp.float32) * (2.0 * math.pi / length)
    return (jnp.cos(angle_rad), jnp.sin(angle_rad))


def deposit_group(total, quad_group, cell_group, row_count, depth):
    flat_cells = cell_group.reshape(-1)
    row_index = flat_cells // depth
    depth_index = flat_cells % depth
    row_hot = (row_index[None, :] == jnp.arange(row_count, dtype=jnp.int32)[:, None]).astype(
        jnp.bfloat16
    )
    depth_hot = (depth_index[:, None] == jnp.arange(depth, dtype=jnp.int32)[None, :]).astype(
        jnp.bfloat16
    )
    values = jnp.transpose(quad_group, (0, 2, 1)).reshape(-1, 6)
    spread = (values[:, :, None] * depth_hot[:, None, :]).reshape(-1, 6 * depth)
    return total + jnp.dot(row_hot, spread, preferred_element_type=jnp.float32)


def line_product(matrix, fields):
    return jnp.einsum("qy,fxyz->fxqz", matrix, fields, precision=lax.Precision.HIGHEST)


def shards(offsets, weights, owners, cells):
    width_x = lax.axis_size("gx")
    width_y = lax.axis_size("gy")
    devices = width_x * width_y
    blocks = owners.shape[0]
    block_pts = cells.shape[0] // blocks
    slot_count = devices * CAP
    quadratic = quad_terms(offsets, weights)
    quad_blocks = jnp.transpose(quadratic.reshape(6, blocks, block_pts), (1, 0, 2))
    cell_blocks = cells.reshape(blocks, block_pts)
    target = owners[:, 0]
    target_hot = (target[:, None] == jnp.arange(devices, dtype=jnp.int32)[None, :]).astype(
        jnp.int32
    )
    earlier = jnp.cumsum(target_hot, axis=0) - target_hot
    rank_in_target = jnp.sum(earlier * target_hot, axis=1)
    slot_index = target * CAP + rank_in_target
    send_quad = jnp.zeros((slot_count, 6, block_pts), jnp.bfloat16).at[slot_index].set(quad_blocks)
    send_cells = jnp.full((slot_count, block_pts), -1, jnp.int32).at[slot_index].set(cell_blocks)
    recv_quad, recv_cells = (
        lax.all_to_all(send_quad, ("gx", "gy"), split_axis=0, concat_axis=0, tiled=True),
        lax.all_to_all(send_cells, ("gx", "gy"), split_axis=0, concat_axis=0, tiled=True),
    )
    group_size = math.gcd(slot_count, max(1, 2048 // block_pts))
    zero_acc = jnp.zeros((CX * CY, 6 * NZ), jnp.float32)

    def step_every(total, pieces):
        return (deposit_group(total, pieces[0], pieces[1], CX * CY, NZ), None)

    accum, ignored = lax.scan(
        step_every,
        zero_acc,
        (
            recv_quad.reshape(slot_count // group_size, group_size, 6, block_pts),
            recv_cells.reshape(slot_count // group_size, group_size, block_pts),
        ),
    )
    fields = jnp.transpose(accum.reshape(CX, CY, 6, NZ), (2, 0, 1, 3))
    sections = width_y.bit_length() - 1
    position = lax.axis_index("gy")
    real_part = fields
    imag_part = jnp.zeros_like(fields)
    for section in range(sections):
        bit_place = sections - 1 - section
        half_span = 1 << bit_place
        is_upper = position & half_span != 0
        within = position % half_span
        angle_rad = within.astype(jnp.float32) * (math.pi / half_span)
        cosine = jnp.cos(angle_rad)
        sine_part = jnp.sin(angle_rad)
        if section == 0:
            other_real = swapped(real_part, "gy", bit_place)
            difference = other_real - real_part
            imag_part = jnp.where(is_upper, -difference * sine_part, jnp.zeros_like(real_part))
            real_part = jnp.where(is_upper, difference * cosine, real_part + other_real)
        else:
            other_real, other_imag = swapped((real_part, imag_part), "gy", bit_place)
            diff_real = other_real - real_part
            diff_imag = other_imag - imag_part
            new_real = jnp.where(
                is_upper, diff_real * cosine + diff_imag * sine_part, real_part + other_real
            )
            new_imag = jnp.where(
                is_upper, diff_imag * cosine - diff_real * sine_part, imag_part + other_imag
            )
            real_part = new_real
            imag_part = new_imag
    length = CY * width_y
    reversed_index = flip_bits(position, sections)
    local_rows = jnp.arange(CY, dtype=jnp.int32)
    phase_int = local_rows * reversed_index % length
    twist_angle = phase_int.astype(jnp.float32) * (2.0 * math.pi / length)
    twist_cos = jnp.cos(twist_angle)[None, None, :, None]
    twist_sin = jnp.sin(twist_angle)[None, None, :, None]
    twist_real = real_part * twist_cos + imag_part * twist_sin
    twist_imag = imag_part * twist_cos - real_part * twist_sin
    cosine, sine_part = rotation(local_rows, local_rows, CY)
    real_out = line_product(cosine, twist_real) + line_product(sine_part, twist_imag)
    imag_out = line_product(cosine, twist_imag) - line_product(sine_part, twist_real)
    return jnp.stack([real_out, imag_out])


def solution(mesh):
    placed = (P(None, ("gx", "gy")), P(("gx", "gy")), P(("gx", "gy"), None), P(("gx", "gy")))
    return jax.shard_map(
        shards,
        mesh=mesh,
        in_specs=placed,
        out_specs=P(None, None, "gx", "gy", None),
        check_vma=False,
    )
```

profile of v0, /device:TPU:0, one launch (start us, length us, event | category | flops | bytes accessed | tf_op | source)
XLA Modules:
  0.0 417.3 jit_solution(8872869091615128708)
XLA Ops:
  3.9 13.3 %scatter_fusion = bf16[256,6,128]{2,1,0:T(8,128)(2,1)} fusion(bf16[256,6,128]{2,1,0:T(8,128)(2,1)} %broadcast_in_dim.10, s32[128]{0:T(128)S(1)} %fusion.42, bf16[128,6,128]{2,1,0:T(8,128)(2,1)S(1)} %copy.39), kind=kCustom, calls=%fused_computation.1 | custom fusion | bytes 590336 | tf_op jit(solution)/shard_map/scatter | solution.py:84
  17.2 11.2 %all-to-all-start.1 = ((bf16[256,6,128]{2,1,0:T(8,128)(2,1)}), bf16[256,6,128]{2,1,0:T(8,128)(2,1)S(1)}, u32[]{:S(2)}, u32[]{:S(2)}) async-start(bf16[256,6,128]{2,1,0:T(8,128)(2,1)} %scatter_fusion), calls=%async_computation.1 | async-start | bytes 1048576 | tf_op jit(solution)/shard_map/all_to_all | solution.py:87
  29.9 12.1 %all-to-all-done.1 = bf16[256,6,128]{2,1,0:T(8,128)(2,1)S(1)} async-done(((bf16[256,6,128]{2,1,0:T(8,128)(2,1)}), bf16[256,6,128]{2,1,0:T(8,128)(2,1)S(1)}, u32[]{:S(2)}, u32[]{:S(2)}) %all-to-all-start.1) | async-done | bytes 393248 | tf_op jit(solution)/shard_map/all_to_all | solution.py:87
  47.4 8.8 %all-to-all-done = s32[128,2,128]{2,1,0:T(2,128)S(1)} async-done(((s32[128,2,128]{2,1,0:T(2,128)}), s32[128,2,128]{2,1,0:T(2,128)S(1)}, u32[]{:S(2)}, u32[]{:S(2)}) %all-to-all-start) | async-done | bytes 131104 | tf_op jit(solution)/shard_map/all_to_all | solution.py:88
  56.1 90.4 %while.13 = (s32[]{:T(128)}, f32[512,768]{1,0:T(8,128)}, s32[16,16,128]{2,1,0:T(8,128)S(1)}, bf16[16,16,6,128]{3,1,2,0:T(8,128)(2,1)}, s32[]{:T(128)}, /*index=5*/s32[]{:T(128)}) while((s32[]{:T(128)}, f32[512,768]{1,0:T(8,128)}, s32[16,16,128]{2,1,0:T(8,128)S(1)}, bf16[16,16,6,128]{3,1,2,0:T(8,128)(2,1)}, s32[]{:T(128)}, ...), condition=%wide.region_5.6_spmd.clone, body=%wide.region_4.5_spmd.clone.sunk | while | flops 1614596096 | bytes 10661979 | solution.py:96
  61.6 4.6 %select_add_fusion.2 = f32[512,768]{1,0:T(8,128)} fusion(f32[512,768]{1,0:T(8,128)} %get-tuple-element.153, bf16[2048,768]{0,1:T(8,128)(2,1)S(1)} %bitcast.114, s32[2048]{0:T(1024)S(1)} %get-tuple-element.145, pred[]{:T(512)S(6)} %compare.26), kind=kOutput, calls=%fused_computation.5.clone.1 | convolution fusion | flops 1612447744 | bytes 6299649 | tf_op jit(solution)/shard_map/while/body/eval_jaxpr/dot_general | solution.py:60
  67.4 4.6 %select_add_fusion.2 = f32[512,768]{1,0:T(8,128)} fusion(f32[512,768]{1,0:T(8,128)} %get-tuple-element.153, bf16[2048,768]{0,1:T(8,128)(2,1)S(1)} %bitcast.114, s32[2048]{0:T(1024)S(1)} %get-tuple-element.145, pred[]{:T(512)S(6)} %compare.26), kind=kOutput, calls=%fused_computation.5.clone.1 | convolution fusion | flops 1612447744 | bytes 6299649 | tf_op jit(solution)/shard_map/while/body/eval_jaxpr/dot_general | solution.py:60
  73.1 4.6 %select_add_fusion.2 = f32[512,768]{1,0:T(8,128)} fusion(f32[512,768]{1,0:T(8,128)} %get-tuple-element.153, bf16[2048,768]{0,1:T(8,128)(2,1)S(1)} %bitcast.114, s32[2048]{0:T(1024)S(1)} %get-tuple-element.145, pred[]{:T(512)S(6)} %compare.26), kind=kOutput, calls=%fused_computation.5.clone.1 | convolution fusion | flops 1612447744 | bytes 6299649 | tf_op jit(solution)/shard_map/while/body/eval_jaxpr/dot_general | solution.py:60
  78.9 4.6 %select_add_fusion.2 = f32[512,768]{1,0:T(8,128)} fusion(f32[512,768]{1,0:T(8,128)} %get-tuple-element.153, bf16[2048,768]{0,1:T(8,128)(2,1)S(1)} %bitcast.114, s32[2048]{0:T(1024)S(1)} %get-tuple-element.145, pred[]{:T(512)S(6)} %compare.26), kind=kOutput, calls=%fused_computation.5.clone.1 | convolution fusion | flops 1612447744 | bytes 6299649 | tf_op jit(solution)/shard_map/while/body/eval_jaxpr/dot_general | solution.py:60
  84.6 4.6 %select_add_fusion.2 = f32[512,768]{1,0:T(8,128)} fusion(f32[512,768]{1,0:T(8,128)} %get-tuple-element.153, bf16[2048,768]{0,1:T(8,128)(2,1)S(1)} %bitcast.114, s32[2048]{0:T(1024)S(1)} %get-tuple-element.145, pred[]{:T(512)S(6)} %compare.26), kind=kOutput, calls=%fused_computation.5.clone.1 | convolution fusion | flops 1612447744 | bytes 6299649 | tf_op jit(solution)/shard_map/while/body/eval_jaxpr/dot_general | solution.py:60
  90.3 4.6 %select_add_fusion.2 = f32[512,768]{1,0:T(8,128)} fusion(f32[512,768]{1,0:T(8,128)} %get-tuple-element.153, bf16[2048,768]{0,1:T(8,128)(2,1)S(1)} %bitcast.114, s32[2048]{0:T(1024)S(1)} %get-tuple-element.145, pred[]{:T(512)S(6)} %compare.26), kind=kOutput, calls=%fused_computation.5.clone.1 | convolution fusion | flops 1612447744 | bytes 6299649 | tf_op jit(solution)/shard_map/while/body/eval_jaxpr/dot_general | solution.py:60
  96.1 4.6 %select_add_fusion.2 = f32[512,768]{1,0:T(8,128)} fusion(f32[512,768]{1,0:T(8,128)} %get-tuple-element.153, bf16[2048,768]{0,1:T(8,128)(2,1)S(1)} %bitcast.114, s32[2048]{0:T(1024)S(1)} %get-tuple-element.145, pred[]{:T(512)S(6)} %compare.26), kind=kOutput, calls=%fused_computation.5.clone.1 | convolution fusion | flops 1612447744 | bytes 6299649 | tf_op jit(solution)/shard_map/while/body/eval_jaxpr/dot_general | solution.py:60
  101.8 4.6 %select_add_fusion.2 = f32[512,768]{1,0:T(8,128)} fusion(f32[512,768]{1,0:T(8,128)} %get-tuple-element.153, bf16[2048,768]{0,1:T(8,128)(2,1)S(1)} %bitcast.114, s32[2048]{0:T(1024)S(1)} %get-tuple-element.145, pred[]{:T(512)S(6)} %compare.26), kind=kOutput, calls=%fused_computation.5.clone.1 | convolution fusion | flops 1612447744 | bytes 6299649 | tf_op jit(solution)/shard_map/while/body/eval_jaxpr/dot_general | solution.py:60
  107.5 4.6 %select_add_fusion.2 = f32[512,768]{1,0:T(8,128)} fusion(f32[512,768]{1,0:T(8,128)} %get-tuple-element.153, bf16[2048,768]{0,1:T(8,128)(2,1)S(1)} %bitcast.114, s32[2048]{0:T(1024)S(1)} %get-tuple-element.145, pred[]{:T(512)S(6)} %compare.26), kind=kOutput, calls=%fused_computation.5.clone.1 | convolution fusion | flops 1612447744 | bytes 6299649 | tf_op jit(solution)/shard_map/while/body/eval_jaxpr/dot_general | solution.py:60
  113.3 4.6 %select_add_fusion.2 = f32[512,768]{1,0:T(8,128)} fusion(f32[512,768]{1,0:T(8,128)} %get-tuple-element.153, bf16[2048,768]{0,1:T(8,128)(2,1)S(1)} %bitcast.114, s32[2048]{0:T(1024)S(1)} %get-tuple-element.145, pred[]{:T(512)S(6)} %compare.26), kind=kOutput, calls=%fused_computation.5.clone.1 | convolution fusion | flops 1612447744 | bytes 6299649 | tf_op jit(solution)/shard_map/while/body/eval_jaxpr/dot_general | solution.py:60
  119.0 4.6 %select_add_fusion.2 = f32[512,768]{1,0:T(8,128)} fusion(f32[512,768]{1,0:T(8,128)} %get-tuple-element.153, bf16[2048,768]{0,1:T(8,128)(2,1)S(1)} %bitcast.114, s32[2048]{0:T(1024)S(1)} %get-tuple-element.145, pred[]{:T(512)S(6)} %compare.26), kind=kOutput, calls=%fused_computation.5.clone.1 | convolution fusion | flops 1612447744 | bytes 6299649 | tf_op jit(solution)/shard_map/while/body/eval_jaxpr/dot_general | solution.py:60
  124.7 4.6 %select_add_fusion.2 = f32[512,768]{1,0:T(8,128)} fusion(f32[512,768]{1,0:T(8,128)} %get-tuple-element.153, bf16[2048,768]{0,1:T(8,128)(2,1)S(1)} %bitcast.114, s32[2048]{0:T(1024)S(1)} %get-tuple-element.145, pred[]{:T(512)S(6)} %compare.26), kind=kOutput, calls=%fused_computation.5.clone.1 | convolution fusion | flops 1612447744 | bytes 6299649 | tf_op jit(solution)/shard_map/while/body/eval_jaxpr/dot_general | solution.py:60
  150.7 36.8 %collective-permute-done = f32[6,8,64,128]{3,2,1,0:T(8,128)} collective-permute-done((f32[6,8,64,128]{3,2,1,0:T(8,128)}, f32[6,8,64,128]{3,2,1,0:T(8,128)}, u32[]{:S(2)}, u32[]{:S(2)}) %collective-permute-start) | collective-permute-done | bytes 1572896 | tf_op jit(solution)/shard_map/ppermute | solution.py:15
  193.3 35.3 %collective-permute-done.1 = f32[6,8,64,128]{3,2,1,0:T(8,128)S(1)} collective-permute-done((f32[6,8,64,128]{3,2,1,0:T(8,128)}, f32[6,8,64,128]{3,2,1,0:T(8,128)S(1)}, u32[]{:S(2)}, u32[]{:S(2)}) %collective-permute-start.1) | collective-permute-done | bytes 1572896 | tf_op jit(solution)/shard_map/ppermute | solution.py:15
  229.7 30.8 %collective-permute-done.2 = f32[6,8,64,128]{3,2,1,0:T(8,128)} collective-permute-done((f32[6,8,64,128]{3,2,1,0:T(8,128)}, f32[6,8,64,128]{3,2,1,0:T(8,128)}, u32[]{:S(2)}, u32[]{:S(2)}) %collective-permute-start.2) | collective-permute-done | bytes 1572896 | tf_op jit(solution)/shard_map/ppermute | solution.py:15
  267.9 35.2 %collective-permute-done.3 = f32[6,8,64,128]{3,2,1,0:T(8,128)} collective-permute-done((f32[6,8,64,128]{3,2,1,0:T(8,128)S(1)}, f32[6,8,64,128]{3,2,1,0:T(8,128)}, u32[]{:S(2)}, u32[]{:S(2)}) %collective-permute-start.3) | collective-permute-done | bytes 1572896 | tf_op jit(solution)/shard_map/ppermute | solution.py:15
  303.1 30.9 %collective-permute-done.4 = f32[6,8,64,128]{3,2,1,0:T(8,128)} collective-permute-done((f32[6,8,64,128]{3,2,1,0:T(8,128)S(1)}, f32[6,8,64,128]{3,2,1,0:T(8,128)}, u32[]{:S(2)}, u32[]{:S(2)}) %collective-permute-start.4) | collective-permute-done | bytes 1572896 | tf_op jit(solution)/shard_map/ppermute | solution.py:15
  339.8 35.3 %collective-permute-done.5 = f32[6,8,64,128]{3,2,1,0:T(8,128)} collective-permute-done((f32[6,8,64,128]{3,2,1,0:T(8,128)S(1)}, f32[6,8,64,128]{3,2,1,0:T(8,128)}, u32[]{:S(2)}, u32[]{:S(2)}) %collective-permute-start.5) | collective-permute-done | bytes 1572896 | tf_op jit(solution)/shard_map/ppermute | solution.py:15
  375.0 30.1 %collective-permute-done.6 = f32[6,8,64,128]{3,2,1,0:T(8,128)} collective-permute-done((f32[6,8,64,128]{3,2,1,0:T(8,128)S(1)}, f32[6,8,64,128]{3,2,1,0:T(8,128)}, u32[]{:S(2)}, u32[]{:S(2)}) %collective-permute-start.6) | collective-permute-done | bytes 1572896 | tf_op jit(solution)/shard_map/ppermute | solution.py:15
  (146 shorter events, 81.9 us)
Async XLA Ops:
  0.0 28.4 %copy-start = (s32[16384]{0:T(1024)S(1)}, s32[16384]{0:T(1024)}, u32[]{:S(2)}) copy-start(s32[16384]{0:T(1024)} %param.9) | copy-start | bytes 196612
  0.0 2.6 copy-start.4
  17.2 24.8 %all-to-all-start.1 = ((bf16[256,6,128]{2,1,0:T(8,128)(2,1)}), bf16[256,6,128]{2,1,0:T(8,128)(2,1)S(1)}, u32[]{:S(2)}, u32[]{:S(2)}) async-start(bf16[256,6,128]{2,1,0:T(8,128)(2,1)} %scatter_fusion), calls=%async_computation.1 | async-start | bytes 1048576 | tf_op jit(solution)/shard_map/all_to_all | solution.py:87
  42.0 14.1 %all-to-all-start = ((s32[128,2,128]{2,1,0:T(2,128)}), s32[128,2,128]{2,1,0:T(2,128)S(1)}, u32[]{:S(2)}, u32[]{:S(2)}) async-start(s32[128,2,128]{2,1,0:T(2,128)} %bitcast.4), calls=%async_computation | async-start | bytes 262144 | tf_op jit(solution)/shard_map/all_to_all | solution.py:88
  149.4 38.0 %collective-permute-start = (f32[6,8,64,128]{3,2,1,0:T(8,128)}, f32[6,8,64,128]{3,2,1,0:T(8,128)}, u32[]{:S(2)}, u32[]{:S(2)}) collective-permute-start(f32[6,8,64,128]{3,2,1,0:T(8,128)} %bitcast.101), channel_id=1, source_target_pairs={{0,8},{1,9},{2,10},{3,11},{4,12},{5,13},{6,14},{7,15},{8,0},{9,1},... | collective-permute-start | bytes 4718600 | tf_op jit(solution)/shard_map/ppermute | solution.py:15
  191.1 37.5 %collective-permute-start.1 = (f32[6,8,64,128]{3,2,1,0:T(8,128)}, f32[6,8,64,128]{3,2,1,0:T(8,128)S(1)}, u32[]{:S(2)}, u32[]{:S(2)}) collective-permute-start(f32[6,8,64,128]{3,2,1,0:T(8,128)} %get-tuple-element.107), channel_id=1, source_target_pairs={{0,4},{1,5},{2,6},{3,7},{4,0},{5,1},{6,2},{7,3},{8,12},{9,13},{10,... | collective-permute-start | bytes 4718600 | tf_op jit(solution)/shard_map/ppermute | solution.py:15
  191.8 68.7 %collective-permute-start.2 = (f32[6,8,64,128]{3,2,1,0:T(8,128)}, f32[6,8,64,128]{3,2,1,0:T(8,128)}, u32[]{:S(2)}, u32[]{:S(2)}) collective-permute-start(f32[6,8,64,128]{3,2,1,0:T(8,128)} %get-tuple-element.108), channel_id=1, source_target_pairs={{0,4},{1,5},{2,6},{3,7},{4,0},{5,1},{6,2},{7,3},{8,12},{9,13},{10,... | collective-permute-start | bytes 4718600 | tf_op jit(solution)/shard_map/ppermute | solution.py:15
  228.6 1.1 copy-start.3
  264.1 39.0 %copy-start.1 = (f32[6,8,64,128]{3,2,1,0:T(8,128)}, f32[6,8,64,128]{3,2,1,0:T(8,128)S(1)}, u32[]{:S(2)}) copy-start(f32[6,8,64,128]{3,2,1,0:T(8,128)S(1)} %get-tuple-element.105) | copy-start | bytes 4718596
  264.1 39.0 %copy-start.2 = (f32[6,8,64,128]{3,2,1,0:T(8,128)}, f32[6,8,64,128]{3,2,1,0:T(8,128)S(1)}, u32[]{:S(2)}) copy-start(f32[6,8,64,128]{3,2,1,0:T(8,128)S(1)} %get-tuple-element.106) | copy-start | bytes 4718596
  264.1 39.0 %collective-permute-start.3 = (f32[6,8,64,128]{3,2,1,0:T(8,128)S(1)}, f32[6,8,64,128]{3,2,1,0:T(8,128)}, u32[]{:S(2)}, u32[]{:S(2)}) collective-permute-start(f32[6,8,64,128]{3,2,1,0:T(8,128)S(1)} %get-tuple-element.105), channel_id=1, source_target_pairs={{0,2},{1,3},{2,0},{3,1},{4,6},{5,7},{6,4},{7,5},{8,10},{9,11},{10,... | collective-permute-start | bytes 4718600 | tf_op jit(solution)/shard_map/ppermute | solution.py:15
  265.5 68.5 %collective-permute-start.4 = (f32[6,8,64,128]{3,2,1,0:T(8,128)S(1)}, f32[6,8,64,128]{3,2,1,0:T(8,128)}, u32[]{:S(2)}, u32[]{:S(2)}) collective-permute-start(f32[6,8,64,128]{3,2,1,0:T(8,128)S(1)} %get-tuple-element.106), channel_id=1, source_target_pairs={{0,2},{1,3},{2,0},{3,1},{4,6},{5,7},{6,4},{7,5},{8,10},{9,11},{10,... | collective-permute-start | bytes 4718600 | tf_op jit(solution)/shard_map/ppermute | solution.py:15
  337.6 37.5 %collective-permute-start.5 = (f32[6,8,64,128]{3,2,1,0:T(8,128)S(1)}, f32[6,8,64,128]{3,2,1,0:T(8,128)}, u32[]{:S(2)}, u32[]{:S(2)}) collective-permute-start(f32[6,8,64,128]{3,2,1,0:T(8,128)S(1)} %get-tuple-element.103), channel_id=1, source_target_pairs={{0,1},{1,0},{2,3},{3,2},{4,5},{5,4},{6,7},{7,6},{8,9},{9,8},{10,11... | collective-permute-start | bytes 4718600 | tf_op jit(solution)/shard_map/ppermute | solution.py:15
  338.2 66.9 %collective-permute-start.6 = (f32[6,8,64,128]{3,2,1,0:T(8,128)S(1)}, f32[6,8,64,128]{3,2,1,0:T(8,128)}, u32[]{:S(2)}, u32[]{:S(2)}) collective-permute-start(f32[6,8,64,128]{3,2,1,0:T(8,128)S(1)} %get-tuple-element.104), channel_id=1, source_target_pairs={{0,1},{1,0},{2,3},{3,2},{4,5},{5,4},{6,7},{7,6},{8,9},{9,8},{10,11... | collective-permute-start | bytes 4718600 | tf_op jit(solution)/shard_map/ppermute | solution.py:15
where the time goes:
time: 419 us; the launch traced here: 417 us
  waiting for transfers between devices  255 us (61%)
  matrix products  79.1 us (19%)
  local copies, waits for them, and re-layouts  32.8 us (8%)
  other arithmetic  24.6 us (6%)
  starting transfers between devices  24.6 us (6%)
    ppermute x7, waiting for transfers between devices, swapped(): lax.ppermute(value, axis, [(i, i ^ 1 << apart) for i in range(lax.axis_si...  234 us
    dot_general x16, matrix products, deposit_group(): return total + jnp.dot(row_hot, spread, preferred_element_type=jnp.float32)  71.5 us
    scatter x1, local copies, waits for them, and re-layouts, shards(): jnp.zeros((slot_count, 6, block_pts), jnp.bfloat16).at[slot_index]  13.3 us
    while x32, local copies, waits for them, and re-layouts  12.1 us
    all_to_all x1, waiting for transfers between devices, shards(): lax.all_to_all(send_quad, ('gx', 'gy'), split_axis=0, concat_axis=0, tile...  12.1 us
    all_to_all x1, starting transfers between devices, shards(): lax.all_to_all(send_quad, ('gx', 'gy'), split_axis=0, concat_axis=0, tile...  11.2 us
    select_n x3, other arithmetic, shards(): jnp.where(is_upper, diff_real * cosine + diff_imag * sine_part, real_part...  9.83 us
    ppermute x7, starting transfers between devices, swapped(): lax.ppermute(value, axis, [(i, i ^ 1 << apart) for i in range(lax.axis_si...  8.83 us
  transfers between devices with their start and end apart: 9, of which 9 were waited for; matrix products, arithmetic and copies ran while one was open for 1% of the time, Pallas kernels for 0%

commit v1 on v0

v1 whole, which is shorter than its diff:
```python
import functools
import math

import jax
import jax.numpy as jnp
import numpy as np
from jax import lax
from jax.experimental import pallas as pl
from jax.experimental.pallas import tpu as pltpu
from jax.sharding import PartitionSpec as P

CX = 8
CY = 64
NZ = 128
BP = 128
CAP = 2
NB = 128
N_GX = 8
N_GY = 16
DEVICES = N_GX * N_GY
ROWS = CX * CY
SHARE = ROWS // N_GY
PASSES = 3
LANES = 2 * NZ
MESH = pl.DeviceIdType.MESH
VMEM = pl.BlockSpec(memory_space=pltpu.VMEM)
ANY = pl.BlockSpec(memory_space=pl.ANY)


def reversed4(value):
    return value % 2 * 8 + value // 2 % 2 * 4 + value // 4 % 2 * 2 + value // 8


def pack_kernel(owner_ref, off_ref, weight_ref, cell_ref, send_ref, count_ref):
    def clear_count(i, carry):
        count_ref[i] = 0
        return carry

    lax.fori_loop(0, DEVICES, clear_count, 0, unroll=8)
    send_ref[...] = jnp.zeros_like(send_ref)
    plane = lax.broadcasted_iota(jnp.int32, (8, BP), 0)
    third = plane % 3

    def block(b, carry):
        owner = owner_ref[b]
        rank = count_ref[owner]
        count_ref[owner] = rank + 1
        lanes = pl.ds(pl.multiple_of(b * BP, BP), BP)
        a = jnp.broadcast_to(off_ref[0:1, lanes], (8, BP))
        bb = jnp.broadcast_to(off_ref[1:2, lanes], (8, BP))
        c = jnp.broadcast_to(off_ref[2:3, lanes], (8, BP))
        w = jnp.broadcast_to(weight_ref[pl.ds(b, 1), :], (8, BP))
        cell = jnp.broadcast_to(cell_ref[pl.ds(b, 1), :], (8, BP))
        scaled = w / jnp.maximum(a * a + bb * bb + c * c, 0.25)
        first = jnp.where(third == 0, a, jnp.where(third == 1, bb, c))
        after = jnp.where(third == 0, bb, jnp.where(third == 1, c, a))
        value = first * jnp.where(plane < 3, first, after) * scaled
        code = jnp.where(plane == 6, cell // NZ - ROWS // 2, cell % NZ).astype(jnp.float32)
        value = jnp.where(plane < 6, value, code)
        send_ref[owner, rank] = value.astype(jnp.bfloat16)
        return carry

    lax.fori_loop(0, NB, block, 0, unroll=4)


def real_transform(values):
    count = len(values)
    if count == 2:
        return [(values[0] + values[1], None), (values[0] - values[1], None)]
    even = real_transform(values[::2])
    odd = real_transform(values[1::2])
    half = count // 2

    def at(spectrum, k):
        if k <= half // 2:
            return spectrum[k]
        re, im = spectrum[half - k]
        return re, None if im is None else -im

    result = []
    for k in range(half + 1):
        ere, eim = at(even, k % half)
        ore, oim = at(odd, k % half)
        if k == 0 or k == half:
            pre, pim = (ore, oim) if k == 0 else (-ore, None if oim is None else -oim)
        elif 4 * k == count:
            pre, pim = (oim, -ore)
        else:
            angle = 2.0 * math.pi * k / count
            cos, sin = math.cos(angle), math.sin(angle)
            if oim is None:
                pre, pim = ore * cos, ore * -sin
            else:
                pre, pim = ore * cos + oim * sin, oim * cos - ore * sin

        def plus(u, v):
            return v if u is None else u if v is None else u + v

        result.append((plus(ere, pre), plus(eim, pim)))
    return result


def exchange_kernel(
    send_ref, out_ref, recv, acc, field, gathered, partial, route_send, route_recv, sends, recvs
):
    gx = lax.axis_index("gx")
    gy = lax.axis_index("gy")
    me = gx * N_GY + gy
    own = pltpu.make_async_copy(send_ref.at[me], recv.at[me], route_recv.at[0])
    own.start()

    def route(j, first):
        to_x = (gx + j) % N_GX

        def one(i, carry):
            to_y = (gy + i) % N_GY
            pltpu.make_async_remote_copy(
                src_ref=send_ref.at[to_x * N_GY + to_y],
                dst_ref=recv.at[me],
                send_sem=route_send,
                recv_sem=route_recv.at[j],
                device_id=(to_x, to_y),
                device_id_type=MESH,
            ).start()
            return carry

        lax.fori_loop(first, N_GY, one, 0)

    route(0, 1)

    def route_all(j, carry):
        route(j, 0)
        return carry

    lax.fori_loop(1, N_GX, route_all, 0)

    row_index = lax.broadcasted_iota(jnp.int32, (ROWS, BP), 0) - ROWS // 2
    row_index = row_index.astype(jnp.float32).astype(jnp.bfloat16)
    depth_index = lax.broadcasted_iota(jnp.int32, (NZ, BP), 0)
    depth_index = depth_index.astype(jnp.float32).astype(jnp.bfloat16)
    one_value = jnp.ones((), jnp.bfloat16)
    zero_value = jnp.zeros((), jnp.bfloat16)

    def deposit(part, j):
        base = (gx + N_GX - j) % N_GX * N_GY
        row_hot, spread = [], []
        for slot in range(N_GY * CAP):
            block = recv[base + slot // CAP, slot % CAP]
            row = jnp.broadcast_to(block[6:7], (ROWS, BP))
            depth = jnp.broadcast_to(block[7:8], (NZ, BP)) == depth_index
            row_hot.append(jnp.where(row == row_index, one_value, zero_value))
            pair = [
                jnp.where(depth, jnp.broadcast_to(block[k : k + 1], (NZ, BP)), zero_value)
                for k in (2 * part, 2 * part + 1)
            ]
            spread.append(jnp.concatenate(pair, axis=0))
        acc[...] += lax.dot_general(
            jnp.concatenate(row_hot, axis=1),
            jnp.concatenate(spread, axis=1),
            (((1,), (1,)), ((), ())),
            preferred_element_type=jnp.float32,
        )

    def scatter_fields(part):
        for i in range(N_GY):
            field[part, i] = acc[i * SHARE : (i + 1) * SHARE].astype(jnp.bfloat16)
        pltpu.make_async_copy(
            field.at[part, gy], gathered.at[part, gy], recvs.at[0, part]
        ).start()

        def one(i, carry):
            to_y = (gy + i) % N_GY
            pltpu.make_async_remote_copy(
                src_ref=field.at[part, to_y],
                dst_ref=gathered.at[part, gy],
                send_sem=sends.at[0, part],
                recv_sem=recvs.at[0, part],
                device_id=(gx, to_y),
                device_id_type=MESH,
            ).start()
            return carry

        lax.fori_loop(1, N_GY, one, 0)

    def frequency_slot(device):
        freq = reversed4(device)
        return 8 - (freq - 8) * (2 * (freq // 8) - 1)

    def transform(part):
        pltpu.make_async_copy(gathered.at[part], gathered.at[part], recvs.at[0, part]).wait()
        for rows in range(SHARE // 16):
            for lanes in range(LANES // 128):
                at = (slice(16 * rows, 16 * rows + 16), slice(128 * lanes, 128 * lanes + 128))
                values = [gathered[(part, s) + at].astype(jnp.float32) for s in range(N_GY)]
                for r, (re, im) in enumerate(real_transform(values)):
                    im = jnp.zeros_like(re) if im is None else im
                    partial[(part, r, 0) + at] = re.astype(jnp.bfloat16)
                    partial[(part, r, 1) + at] = im.astype(jnp.bfloat16)
        pltpu.make_async_copy(
            partial.at[part, frequency_slot(gy)], out_ref.at[part, gy], recvs.at[1, part]
        ).start()

        def one(i, carry):
            to_y = (gy + i) % N_GY
            pltpu.make_async_remote_copy(
                src_ref=partial.at[part, frequency_slot(to_y)],
                dst_ref=out_ref.at[part, gy],
                send_sem=sends.at[1, part],
                recv_sem=recvs.at[1, part],
                device_id=(gx, to_y),
                device_id_type=MESH,
            ).start()
            return carry

        lax.fori_loop(1, N_GY, one, 0)

    for part in range(PASSES):
        acc[...] = jnp.zeros_like(acc)

        def step(j, carry):
            if part == 0:
                arrived = recv.at[pl.ds(0, N_GY)]
                pltpu.make_async_copy(arrived, arrived, route_recv.at[j]).wait()
            deposit(part, j)
            return carry

        if part == 0:
            lax.fori_loop(0, N_GX, step, 0)
        else:
            lax.fori_loop(0, N_GX // 2, step, 0)
            transform(part - 1)
            lax.fori_loop(N_GX // 2, N_GX, step, 0)
        scatter_fields(part)
    transform(PASSES - 1)

    sent = send_ref.at[pl.ds(0, DEVICES - 1)]
    pltpu.make_async_copy(sent, sent, route_send).wait()
    for part in range(PASSES):
        sent = field.at[part, pl.ds(0, N_GY - 1)]
        pltpu.make_async_copy(sent, sent, sends.at[0, part]).wait()
        sent = out_ref.at[part, pl.ds(0, N_GY - 1)]
        pltpu.make_async_copy(sent, sent, sends.at[1, part]).wait()
        pltpu.make_async_copy(out_ref.at[part], out_ref.at[part], recvs.at[1, part]).wait()


def lines_kernel(table_ref, part_ref, out_ref, matrix, sem):
    freq = reversed4(lax.axis_index("gy"))

    @pl.when(pl.program_id(0) == 0)
    def _():
        copy = pltpu.make_async_copy(table_ref.at[freq], matrix, sem)
        copy.start()
        copy.wait()

    for x in range(CX):
        values = part_ref[0, 2 * x : 2 * x + 2].reshape(2 * CY, LANES)
        lines = jnp.dot(matrix[0], values, preferred_element_type=jnp.float32)
        lines += jnp.dot(matrix[1], values, preferred_element_type=jnp.float32)
        for half in range(2):
            for k in range(2):
                out_ref[half, k, x] = lines[half * CY : half * CY + CY, k * NZ : k * NZ + NZ]


def line_table():
    y = np.arange(CY)
    q = np.arange(CY)
    tables = []
    for freq in range(N_GY):
        phase = (q[:, None] * N_GY + freq) * y[None, :] % (CY * N_GY)
        angle = phase * (2.0 * np.pi / (CY * N_GY))
        cos, sin = np.cos(angle), np.sin(angle)
        sign = -1.0 if freq > N_GY // 2 else 1.0
        full = np.stack([np.stack([cos, sign * sin], 1), np.stack([-sin, sign * cos], 1)])
        full = full.reshape(2, CY, 2, 2, CY // 2).transpose(0, 1, 3, 2, 4).reshape(2 * CY, 2 * CY)
        high = full.astype(jnp.bfloat16)
        tables.append(np.stack([high, (full - high.astype(np.float64)).astype(jnp.bfloat16)]))
    return np.stack(tables)


def shards(table, offsets, weights, owners, cells):
    send = pl.pallas_call(
        pack_kernel,
        out_shape=jax.ShapeDtypeStruct((DEVICES, CAP, 8, BP), jnp.bfloat16),
        in_specs=[pl.BlockSpec(memory_space=pltpu.SMEM), VMEM, VMEM, VMEM],
        out_specs=VMEM,
        scratch_shapes=[pltpu.SMEM((DEVICES,), jnp.int32)],
        name="pack",
    )(owners.reshape(NB), offsets, weights.reshape(NB, BP), cells.reshape(NB, BP))
    partial = pl.pallas_call(
        exchange_kernel,
        out_shape=jax.ShapeDtypeStruct((PASSES, N_GY, 2, SHARE, LANES), jnp.bfloat16),
        in_specs=[VMEM],
        out_specs=ANY,
        scratch_shapes=[
            pltpu.VMEM((DEVICES, CAP, 8, BP), jnp.bfloat16),
            pltpu.VMEM((ROWS, LANES), jnp.float32),
            pltpu.VMEM((PASSES, N_GY, SHARE, LANES), jnp.bfloat16),
            pltpu.VMEM((PASSES, N_GY, SHARE, LANES), jnp.bfloat16),
            pltpu.VMEM((PASSES, N_GY // 2 + 1, 2, SHARE, LANES), jnp.bfloat16),
            pltpu.SemaphoreType.DMA,
            pltpu.SemaphoreType.DMA((N_GX,)),
            pltpu.SemaphoreType.DMA((2, PASSES)),
            pltpu.SemaphoreType.DMA((2, PASSES)),
        ],
        compiler_params=pltpu.CompilerParams(has_side_effects=True, vmem_limit_bytes=60 << 20),
        name="exchange",
    )(send)
    return pl.pallas_call(
        lines_kernel,
        grid=(PASSES,),
        out_shape=jax.ShapeDtypeStruct((2, 6, CX, CY, NZ), jnp.float32),
        in_specs=[ANY, pl.BlockSpec((1, N_GY, 2, SHARE, LANES), lambda c: (c, 0, 0, 0, 0))],
        out_specs=pl.BlockSpec((2, 2, CX, CY, NZ), lambda c: (0, c, 0, 0, 0)),
        scratch_shapes=[
            pltpu.VMEM((2, 2 * CY, 2 * CY), jnp.bfloat16),
            pltpu.SemaphoreType.DMA,
        ],
        name="lines",
    )(table, partial)


def solution(mesh):
    table = line_table()
    placed = (P(None, ("gx", "gy")), P(("gx", "gy")), P(("gx", "gy"), None), P(("gx", "gy")))
    mapped = jax.shard_map(
        shards,
        mesh=mesh,
        in_specs=(P(),) + placed,
        out_specs=P(None, None, "gx", "gy", None),
        check_vma=False,
    )
    return functools.partial(mapped, jnp.asarray(table))
```

time: 419 us -> 75.8 us (0.18)
  waiting for transfers between devices: 255 us -> 0 us
  matrix products: 79.1 us -> 0 us
  Pallas kernels: 0 us -> 75 us
  local copies, waits for them, and re-layouts: 32.8 us -> 0 us
  other arithmetic: 24.6 us -> 0 us
  starting transfers between devices: 24.6 us -> 0 us
    ppermute x7 -> x0, waiting for transfers between devices: 234 us -> none  [swapped(): lax.ppermute(value, axis, [(i, i ^ 1 << apart) for i in range(lax.axis_si...]
    dot_general x20 -> x0, matrix products: 79.1 us -> none  [the longest x16 71.5 us: deposit_group(): return total + jnp.dot(row_hot, spread, preferred_element_type=jnp.float32)]
    pallas_call x0 -> x3, Pallas kernels: none -> 75 us  [the longest x1 66.8 us: shards(): pl.pallas_call(exchange_kernel, out_shape=jax.ShapeDtypeStruct((PASSES, N...]
    all_to_all x2 -> x0, waiting for transfers between devices: 20.9 us -> none  [the longest x1 12.1 us: shards(): lax.all_to_all(send_quad, ('gx', 'gy'), split_axis=0, concat_axis=0, tile...]
    all_to_all x2 -> x0, starting transfers between devices: 15.7 us -> none  [the longest x1 11.2 us: shards(): lax.all_to_all(send_quad, ('gx', 'gy'), split_axis=0, concat_axis=0, tile...]
    scatter x2 -> x0, local copies, waits for them, and re-layouts: 14.8 us -> none  [the longest x1 13.3 us: shards(): jnp.zeros((slot_count, 6, block_pts), jnp.bfloat16).at[slot_index]]
    select_n x37 -> x0, other arithmetic: 14 us -> none  [the longest x3 9.83 us: shards(): jnp.where(is_upper, diff_real * cosine + diff_imag * sine_part, real_part...]
    while x32 -> x0, local copies, waits for them, and re-layouts: 12.1 us -> none
  transfers between devices with their start and end apart: 9 -> 0, of which waited for: 9 -> 0; matrix products, arithmetic and copies ran while one was open for 1% -> 0% of each run, Pallas kernels for 0% -> 0%
where the time goes in v1:
time: 75.8 us; the launch traced here: 75 us
  Pallas kernels  75 us (99%)
    pallas_call x1, Pallas kernels, shards(): pl.pallas_call(exchange_kernel, out_shape=jax.ShapeDtypeStruct((PASSES, N...  66.8 us
    pallas_call x1, Pallas kernels, shards(): pl.pallas_call(lines_kernel, grid=(PASSES,), out_shape=jax.ShapeDtypeStru...  5.18 us
    pallas_call x1, Pallas kernels, shards(): pl.pallas_call(pack_kernel, out_shape=jax.ShapeDtypeStruct((DEVICES, CAP,...  2.98 us

profile of v1, /device:TPU:0, one launch (start us, length us, event | category | flops | bytes accessed | tf_op | source)
XLA Modules:
  0.0 75.0 jit_solution(8899919415915810538)
XLA Ops:
  0.0 3.0 %pack.1.send_ref = bf16[128,2,8,128]{3,2,1,0:T(8,128)(2,1)} custom-call(s32[128]{0:T(128)} %bitcast.5, f32[3,16384]{1,0:T(4,128)} %off_ref.1, f32[128,128]{1,0:T(8,128)} %bitcast.3, s32[128,128]{1,0:T(8,128)} %bitcast.4), custom_call_target="tpu_custom_call" | custom-call | tf_op jit(solution)/shard_map/pack/pallas_call | solution.py:281
  3.0 66.8 %exchange.1.part_ref = bf16[3,16,2,32,256]{4,3,2,1,0:T(8,128)(2,1)} custom-call(bf16[128,2,8,128]{3,2,1,0:T(8,128)(2,1)} %pack.1.send_ref), custom_call_target="tpu_custom_call" | custom-call | tf_op jit(solution)/shard_map/exchange/pallas_call | solution.py:289
  69.8 5.2 %lines.1 = f32[2,6,8,64,128]{4,3,2,1,0:T(8,128)} custom-call(bf16[16,2,128,128]{3,2,1,0:T(8,128)(2,1)} %constant.2.clone.table_ref, bf16[3,16,2,32,256]{4,3,2,1,0:T(8,128)(2,1)} %exchange.1.part_ref), custom_call_target="tpu_custom_call" | custom-call | tf_op jit(solution)/shard_map/lines/pallas_call | solution.py:308

commit v2 on v1

v2 whole, which is shorter than its diff:
```python
import functools
import math

import jax
import jax.numpy as jnp
import numpy as np
from jax import lax
from jax.experimental import pallas as pl
from jax.experimental.pallas import tpu as pltpu
from jax.sharding import PartitionSpec as P

CX = 8
CY = 64
NZ = 128
BP = 128
CAP = 2
NB = 128
N_GX = 8
N_GY = 16
DEVICES = N_GX * N_GY
ROWS = CX * CY
LANES = 2 * NZ
GRANULE = 16
UNITS = ((0, 0, ROWS), (1, 0, ROWS), (2, 0, ROWS // 2), (2, ROWS // 2, ROWS // 2))
MESH = pl.DeviceIdType.MESH
ANY = pl.BlockSpec(memory_space=pl.ANY)


def granules(unit):
    return unit[2] // (N_GY * GRANULE)


def reversed4(value):
    return value % 2 * 8 + value // 2 % 2 * 4 + value // 4 % 2 * 2 + value // 8


def real_transform(values):
    count = len(values)
    if count == 2:
        return [(values[0] + values[1], None), (values[0] - values[1], None)]
    even = real_transform(values[::2])
    odd = real_transform(values[1::2])
    half = count // 2

    def at(spectrum, k):
        if k <= half // 2:
            return spectrum[k]
        re, im = spectrum[half - k]
        return re, None if im is None else -im

    result = []
    for k in range(half + 1):
        ere, eim = at(even, k % half)
        ore, oim = at(odd, k % half)
        if k == 0 or k == half:
            pre, pim = (ore, oim) if k == 0 else (-ore, None if oim is None else -oim)
        elif 4 * k == count:
            pre, pim = (oim, -ore)
        else:
            angle = 2.0 * math.pi * k / count
            cos, sin = math.cos(angle), math.sin(angle)
            if oim is None:
                pre, pim = ore * cos, ore * -sin
            else:
                pre, pim = ore * cos + oim * sin, oim * cos - ore * sin

        def plus(u, v):
            return v if u is None else u if v is None else u + v

        result.append((plus(ere, pre), plus(eim, pim)))
    return result


def write_slots(owner, offsets, weights, cells, planes, send_ref):
    a, b, c = (offsets[:, i, :] for i in range(3))
    scaled = weights / jnp.maximum(a * a + b * b + c * c, 0.25)
    pairs = ((a, a), (b, b), (c, c), (a, b), (b, c), (c, a))
    values = [(first * second * scaled).astype(jnp.bfloat16) for first, second in pairs]
    row = (cells >> 7) - ROWS // 2
    values += [code.astype(jnp.float32).astype(jnp.bfloat16) for code in (row, cells & (NZ - 1))]
    across = jnp.broadcast_to(owner.astype(jnp.float32), (NB, NB))
    same = jnp.where(across == across.T, 1.0, 0.0)
    block = lax.broadcasted_iota(jnp.int32, (NB, NB), 0)
    before = jnp.where(block < lax.broadcasted_iota(jnp.int32, (NB, NB), 1), same, 0.0)
    slot = owner.astype(jnp.float32) * CAP + jnp.sum(before, axis=0, keepdims=True)
    slots = lax.broadcasted_iota(jnp.int32, (DEVICES * CAP, NB), 0).astype(jnp.float32)
    hot = jnp.where(slots == slot, 1.0, 0.0).astype(jnp.bfloat16)
    for k, value in enumerate(values):
        placed = jnp.dot(hot, value, preferred_element_type=jnp.float32)
        planes[pl.ds(k, DEVICES * CAP, stride=8), :] = placed
    send_ref[...] = planes[...].reshape(DEVICES, CAP, 8, BP).astype(jnp.bfloat16)


def exchange_kernel(owner_hbm, offset_hbm, weight_hbm, cell_hbm, *refs):
    count = len(UNITS)
    outs, refs = refs[:count], refs[count:]
    fields, refs = refs[:count], refs[count:]
    gathered, refs = refs[:count], refs[count:]
    partials, refs = refs[:count], refs[count:]
    owner_ref, offset_ref, weight_ref, cell_ref, planes, send_ref, recv, acc = refs[:8]
    load_sems, route_send, route_recv, sends, recvs = refs[8:]
    gx = lax.axis_index("gx")
    gy = lax.axis_index("gy")
    me = gx * N_GY + gy

    loads = [
        pltpu.make_async_copy(source, target, load_sems.at[i])
        for i, (source, target) in enumerate(
            (
                (owner_hbm, owner_ref),
                (offset_hbm, offset_ref),
                (weight_hbm, weight_ref),
                (cell_hbm, cell_ref),
            )
        )
    ]
    for load in loads:
        load.start()
    barrier = pltpu.get_barrier_semaphore()

    def greet(i, carry):
        other = (me + i) % DEVICES
        pl.semaphore_signal(
            barrier, inc=1, device_id=(other // N_GY, other % N_GY), device_id_type=MESH
        )
        return carry

    lax.fori_loop(1, DEVICES, greet, 0)
    for load in loads:
        load.wait()
    write_slots(owner_ref[...], offset_ref, weight_ref[...], cell_ref[...], planes, send_ref)
    pl.semaphore_wait(barrier, DEVICES - 1)

    pltpu.make_async_copy(send_ref.at[me], recv.at[me], route_recv.at[0]).start()

    def route(j, first):
        to_x = (gx + j) % N_GX

        def one(i, carry):
            to_y = (gy + i) % N_GY
            pltpu.make_async_remote_copy(
                src_ref=send_ref.at[to_x * N_GY + to_y],
                dst_ref=recv.at[me],
                send_sem=route_send,
                recv_sem=route_recv.at[j],
                device_id=(to_x, to_y),
                device_id_type=MESH,
            ).start()
            return carry

        lax.fori_loop(first, N_GY, one, 0)

    route(0, 1)

    def route_all(j, carry):
        route(j, 0)
        return carry

    lax.fori_loop(1, N_GX, route_all, 0)

    depth_index = lax.broadcasted_iota(jnp.int32, (NZ, BP), 0)
    depth_index = depth_index.astype(jnp.float32).astype(jnp.bfloat16)
    one_value = jnp.ones((), jnp.bfloat16)
    zero_value = jnp.zeros((), jnp.bfloat16)

    def deposit(unit, first, phases):
        pair, low, rows = unit
        row_index = lax.broadcasted_iota(jnp.int32, (rows, BP), 0) + (low - ROWS // 2)
        row_index = row_index.astype(jnp.float32).astype(jnp.bfloat16)
        row_hot, spread = [], []
        for phase in range(phases):
            base = (gx + N_GX - (first + phase)) % N_GX * N_GY
            for slot in range(N_GY * CAP):
                block = recv[base + slot // CAP, slot % CAP]
                row = jnp.broadcast_to(block[6:7], (rows, BP))
                depth = jnp.broadcast_to(block[7:8], (NZ, BP)) == depth_index
                row_hot.append(jnp.where(row == row_index, one_value, zero_value))
                terms = [
                    jnp.where(depth, jnp.broadcast_to(block[k : k + 1], (NZ, BP)), zero_value)
                    for k in (2 * pair, 2 * pair + 1)
                ]
                spread.append(jnp.concatenate(terms, axis=0))
        acc[:rows] += lax.dot_general(
            jnp.concatenate(row_hot, axis=1),
            jnp.concatenate(spread, axis=1),
            (((1,), (1,)), ((), ())),
            preferred_element_type=jnp.float32,
        )

    def to_peers(sources, target, slot_of, stage, unit_index):
        pltpu.make_async_copy(
            sources.at[slot_of(gy)], target.at[gy], recvs.at[stage, unit_index]
        ).start()

        def one(i, carry):
            to_y = (gy + i) % N_GY
            pltpu.make_async_remote_copy(
                src_ref=sources.at[slot_of(to_y)],
                dst_ref=target.at[gy],
                send_sem=sends.at[stage, unit_index],
                recv_sem=recvs.at[stage, unit_index],
                device_id=(gx, to_y),
                device_id_type=MESH,
            ).start()
            return carry

        lax.fori_loop(1, N_GY, one, 0)

    def scatter_fields(u):
        parts = granules(UNITS[u])
        for i in range(N_GY):
            for g in range(parts):
                start = (i * parts + g) * GRANULE
                fields[u][i, g] = acc[start : start + GRANULE].astype(jnp.bfloat16)
        to_peers(fields[u], gathered[u], lambda device: device, 0, u)

    def frequency_slot(device):
        freq = reversed4(device)
        return 8 - (freq - 8) * (2 * (freq // 8) - 1)

    def transform(u):
        pltpu.make_async_copy(gathered[u], gathered[u], recvs.at[0, u]).wait()
        for g in range(granules(UNITS[u])):
            for half in range(LANES // 128):
                lanes = slice(128 * half, 128 * half + 128)
                values = [gathered[u][s, g, :, lanes].astype(jnp.float32) for s in range(N_GY)]
                for r, (re, im) in enumerate(real_transform(values)):
                    im = jnp.zeros_like(re) if im is None else im
                    partials[u][r, g, 0, :, lanes] = re.astype(jnp.bfloat16)
                    partials[u][r, g, 1, :, lanes] = im.astype(jnp.bfloat16)
        to_peers(partials[u], outs[u], frequency_slot, 1, u)

    def run(u, first, last, phases):
        def step(i, carry):
            if u == 0:
                arrived = recv.at[pl.ds(0, N_GY)]
                pltpu.make_async_copy(arrived, arrived, route_recv.at[i]).wait()
            deposit(UNITS[u], i * phases, phases)
            return carry

        lax.fori_loop(first // phases, last // phases, step, 0)

    for u in range(count):
        acc[...] = jnp.zeros_like(acc)
        if u == 0:
            run(u, 0, N_GX, 1)
        elif u == 2:
            run(u, 0, N_GX, 2)
        else:
            run(u, 0, N_GX // 2, 2)
            transform(u - 1)
            run(u, N_GX // 2, N_GX, 2)
        scatter_fields(u)
        if u == 2:
            transform(u - 1)
    transform(count - 1)

    sent = send_ref.at[pl.ds(0, DEVICES - 1)]
    pltpu.make_async_copy(sent, sent, route_send).wait()
    for u in range(count):
        sent = fields[u].at[pl.ds(0, N_GY - 1)]
        pltpu.make_async_copy(sent, sent, sends.at[0, u]).wait()
        sent = outs[u].at[pl.ds(0, N_GY - 1)]
        pltpu.make_async_copy(sent, sent, sends.at[1, u]).wait()
        pltpu.make_async_copy(outs[u], outs[u], recvs.at[1, u]).wait()


def lines_kernel(table_ref, *refs):
    count = len(UNITS)
    parts, refs = refs[:count], refs[count:]
    out_ref, refs = refs[0], refs[1:]
    held, refs = refs[:count], refs[count:]
    matrix, staged, load_sems, store_sem = refs
    freq = reversed4(lax.axis_index("gy"))
    loads = [pltpu.make_async_copy(table_ref.at[freq], matrix, load_sems.at[count])]
    loads += [pltpu.make_async_copy(parts[u], held[u], load_sems.at[u]) for u in range(count)]
    for load in loads:
        load.start()
    loads[0].wait()
    for u, (pair, low, rows) in enumerate(UNITS):
        loads[1 + u].wait()
        sources = N_GY * CY // rows
        for x in range(rows // CY):
            values = held[u][sources * x : sources * x + sources].reshape(2 * CY, LANES)
            lines = jnp.dot(matrix[0], values, preferred_element_type=jnp.float32)
            lines += jnp.dot(matrix[1], values, preferred_element_type=jnp.float32)
            to_x = low // CY + x
            for half in range(2):
                for k in range(2):
                    staged[half, 2 * pair + k, to_x] = lines[
                        half * CY : half * CY + CY, k * NZ : k * NZ + NZ
                    ]
            if x % 4 == 3:
                for half in range(2):
                    at = (half, pl.ds(2 * pair, 2), pl.ds(to_x - 3, 4))
                    pltpu.make_async_copy(staged.at[at], out_ref.at[at], store_sem).start()
    pltpu.make_async_copy(staged, out_ref, store_sem).wait()


def line_table():
    y = np.arange(CY)
    q = np.arange(CY)
    tables = []
    for freq in range(N_GY):
        phase = (q[:, None] * N_GY + freq) * y[None, :] % (CY * N_GY)
        angle = phase * (2.0 * np.pi / (CY * N_GY))
        cos, sin = np.cos(angle), np.sin(angle)
        sign = -1.0 if freq > N_GY // 2 else 1.0
        full = np.stack([np.stack([cos, sign * sin], 1), np.stack([-sin, sign * cos], 1)])
        full = full.reshape(2, CY, 2, CY // GRANULE, GRANULE).transpose(0, 1, 3, 2, 4)
        full = full.reshape(2 * CY, 2 * CY)
        high = full.astype(jnp.bfloat16)
        tables.append(np.stack([high, (full - high.astype(np.float64)).astype(jnp.bfloat16)]))
    return np.stack(tables)


def shards(table, offsets, weights, owners, cells):
    unit_shapes = [(N_GY, granules(unit), GRANULE, LANES) for unit in UNITS]
    half_shapes = [(9, granules(unit), 2, GRANULE, LANES) for unit in UNITS]
    out_shapes = [(N_GY, granules(unit), 2, GRANULE, LANES) for unit in UNITS]
    parts = pl.pallas_call(
        exchange_kernel,
        out_shape=[jax.ShapeDtypeStruct(shape, jnp.bfloat16) for shape in out_shapes],
        in_specs=[ANY] * 4,
        out_specs=[ANY] * len(UNITS),
        scratch_shapes=[
            *[pltpu.VMEM(shape, jnp.bfloat16) for shape in unit_shapes],
            *[pltpu.VMEM(shape, jnp.bfloat16) for shape in unit_shapes],
            *[pltpu.VMEM(shape, jnp.bfloat16) for shape in half_shapes],
            pltpu.VMEM((1, NB), jnp.int32),
            pltpu.VMEM((NB, 3, BP), jnp.float32),
            pltpu.VMEM((NB, BP), jnp.float32),
            pltpu.VMEM((NB, BP), jnp.int32),
            pltpu.VMEM((DEVICES * CAP * 8, BP), jnp.float32),
            pltpu.VMEM((DEVICES, CAP, 8, BP), jnp.bfloat16),
            pltpu.VMEM((DEVICES, CAP, 8, BP), jnp.bfloat16),
            pltpu.VMEM((ROWS, LANES), jnp.float32),
            pltpu.SemaphoreType.DMA((4,)),
            pltpu.SemaphoreType.DMA,
            pltpu.SemaphoreType.DMA((N_GX,)),
            pltpu.SemaphoreType.DMA((2, len(UNITS))),
            pltpu.SemaphoreType.DMA((2, len(UNITS))),
        ],
        compiler_params=pltpu.CompilerParams(
            has_side_effects=True, collective_id=0, vmem_limit_bytes=60 << 20
        ),
        name="exchange",
    )(
        owners.reshape(1, NB),
        jnp.transpose(offsets.reshape(3, NB, BP), (1, 0, 2)),
        weights.reshape(NB, BP),
        cells.reshape(NB, BP),
    )
    return pl.pallas_call(
        lines_kernel,
        out_shape=jax.ShapeDtypeStruct((2, 6, CX, CY, NZ), jnp.float32),
        in_specs=[ANY] * (1 + len(UNITS)),
        out_specs=ANY,
        scratch_shapes=[
            *[pltpu.VMEM(shape, jnp.bfloat16) for shape in out_shapes],
            pltpu.VMEM((2, 2 * CY, 2 * CY), jnp.bfloat16),
            pltpu.VMEM((2, 6, CX, CY, NZ), jnp.float32),
            pltpu.SemaphoreType.DMA((1 + len(UNITS),)),
            pltpu.SemaphoreType.DMA,
        ],
        name="lines",
    )(table, *parts)


def solution(mesh):
    table = line_table()
    placed = (P(None, ("gx", "gy")), P(("gx", "gy")), P(("gx", "gy"), None), P(("gx", "gy")))
    mapped = jax.shard_map(
        shards,
        mesh=mesh,
        in_specs=(P(),) + placed,
        out_specs=P(None, None, "gx", "gy", None),
        check_vma=False,
    )
    return functools.partial(mapped, jnp.asarray(table))
```

time: 75.8 us -> 66.2 us (0.87); the launches traced: 75 us -> 66.1 us
  Pallas kernels: 75 us -> 66.1 us
    pallas_call x3 -> x2, Pallas kernels: 75 us -> 66.1 us  [the longest x1 62.8 us: shards(): pl.pallas_call(exchange_kernel, out_shape=[jax.ShapeDtypeStruct(shape, jn...]
where the time goes in v2:
time: 66.2 us; the launch traced here: 66.1 us
  Pallas kernels  66.1 us (100%)
    pallas_call x1, Pallas kernels, shards(): pl.pallas_call(exchange_kernel, out_shape=[jax.ShapeDtypeStruct(shape, jn...  62.8 us
    pallas_call x1, Pallas kernels, shards(): pl.pallas_call(lines_kernel, out_shape=jax.ShapeDtypeStruct((2, 6, CX, CY...  3.36 us

profile of v2, /device:TPU:0, one launch (start us, length us, event | category | flops | bytes accessed | tf_op | source)
XLA Modules:
  0.0 66.1 jit_solution(7426063886215312664)
XLA Ops:
  0.0 62.8 %exchange.1 = (bf16[16,2,2,16,256]{4,3,2,1,0:T(8,128)(2,1)}, bf16[16,2,2,16,256]{4,3,2,1,0:T(8,128)(2,1)}, bf16[16,1,2,16,256]{4,3,2,1,0:T(8,128)(2,1)}, bf16[16,1,2,16,256]{4,3,2,1,0:T(8,128)(2,1)}) custom-call(s32[1,128]{1,0:T(1,128)} %bitcast.9, f32[128,3,128]{2,1,0:T(4,128)} %bitcast.6, f32[128,128]{1,0:T(8,128)} %bitcast.7, s32[128,128]{1,0:T(8,128)} %bitcast.8), custom_call_target="tpu_custom_call" | custom-call | tf_op jit(solution)/shard_map/exchange/pallas_call | solution.py:321
  62.8 3.4 %lines.1 = f32[2,6,8,64,128]{4,3,2,1,0:T(8,128)} custom-call(bf16[16,2,128,128]{3,2,1,0:T(8,128)(2,1)} %constant.2.clone.table_ref, bf16[16,2,2,16,256]{4,3,2,1,0:T(8,128)(2,1)} %get-tuple-element.9.refs_0_, bf16[16,2,2,16,256]{4,3,2,1,0:T(8,128)(2,1)} %get-tuple-element.10.refs_1_, bf16[16,1,2,16,256]{4,3,2,1,0:T(8,128)(2,1)} %get-tuple-element.11.refs_2_, ...), custom_call_target="tpu_custom_call" | custom-call | tf_op jit(solution)/shard_map/lines/pallas_call | solution.py:354

commit v3 on v2

--- a/solution.py
+++ b/solution.py
@@ -21,13 +21,20 @@
 ROWS = CX * CY
 LANES = 2 * NZ
 GRANULE = 16
-UNITS = ((0, 0, ROWS), (1, 0, ROWS), (2, 0, ROWS // 2), (2, ROWS // 2, ROWS // 2))
+HALF = ROWS // 2
+UNITS = ((0, 0, HALF), (0, HALF, HALF), (1, 0, ROWS), (2, 0, HALF), (2, HALF, HALF))
 MESH = pl.DeviceIdType.MESH
 ANY = pl.BlockSpec(memory_space=pl.ANY)
+HBM = pl.BlockSpec(memory_space=pltpu.HBM)
+VMEM = pl.BlockSpec(memory_space=pltpu.VMEM)
 
 
 def granules(unit):
     return unit[2] // (N_GY * GRANULE)
+
+
+def far_first(k, count):
+    return count // 2 + (1 - 2 * (k % 2)) * ((k + 1) // 2)
 
 
 def reversed4(value):
@@ -91,9 +98,10 @@
     send_ref[...] = planes[...].reshape(DEVICES, CAP, 8, BP).astype(jnp.bfloat16)
 
 
-def exchange_kernel(owner_hbm, offset_hbm, weight_hbm, cell_hbm, *refs):
+def exchange_kernel(owner_hbm, offset_hbm, weight_hbm, cell_hbm, table_hbm, *refs):
     count = len(UNITS)
     outs, refs = refs[:count], refs[count:]
+    matrix_ref, refs = refs[0], refs[1:]
     fields, refs = refs[:count], refs[count:]
     gathered, refs = refs[:count], refs[count:]
     partials, refs = refs[:count], refs[count:]
@@ -116,16 +124,19 @@
     ]
     for load in loads:
         load.start()
+    matrix_load = pltpu.make_async_copy(
+        table_hbm.at[reversed4(gy)], matrix_ref, load_sems.at[len(loads)]
+    )
+    matrix_load.start()
     barrier = pltpu.get_barrier_semaphore()
 
     def greet(i, carry):
-        other = (me + i) % DEVICES
-        pl.semaphore_signal(
-            barrier, inc=1, device_id=(other // N_GY, other % N_GY), device_id_type=MESH
-        )
+        to_x = (gx + far_first(i // N_GY, N_GX)) % N_GX
+        to_y = (gy + far_first(i % N_GY, N_GY)) % N_GY
+        pl.semaphore_signal(barrier, inc=1, device_id=(to_x, to_y), device_id_type=MESH)
         return carry
 
-    lax.fori_loop(1, DEVICES, greet, 0)
+    lax.fori_loop(0, DEVICES - 1, greet, 0)
     for load in loads:
         load.wait()
     write_slots(owner_ref[...], offset_ref, weight_ref[...], cell_ref[...], planes, send_ref)
@@ -133,11 +144,11 @@
 
     pltpu.make_async_copy(send_ref.at[me], recv.at[me], route_recv.at[0]).start()
 
-    def route(j, first):
+    def route(j, last):
         to_x = (gx + j) % N_GX
 
         def one(i, carry):
-            to_y = (gy + i) % N_GY
+            to_y = (gy + far_first(i, N_GY)) % N_GY
             pltpu.make_async_remote_copy(
                 src_ref=send_ref.at[to_x * N_GY + to_y],
                 dst_ref=recv.at[me],
@@ -148,12 +159,12 @@
             ).start()
             return carry
 
-        lax.fori_loop(first, N_GY, one, 0)
-
-    route(0, 1)
+        lax.fori_loop(0, last, one, 0)
+
+    route(0, N_GY - 1)
 
     def route_all(j, carry):
-        route(j, 0)
+        route(j, N_GY)
         return carry
 
     lax.fori_loop(1, N_GX, route_all, 0)
@@ -163,8 +174,7 @@
     one_value = jnp.ones((), jnp.bfloat16)
     zero_value = jnp.zeros((), jnp.bfloat16)
 
-    def deposit(unit, first, phases):
-        pair, low, rows = unit
+    def deposit(pair, low, rows, first, phases):
         row_index = lax.broadcasted_iota(jnp.int32, (rows, BP), 0) + (low - ROWS // 2)
         row_index = row_index.astype(jnp.float32).astype(jnp.bfloat16)
         row_hot, spread = [], []
@@ -180,7 +190,7 @@
                     for k in (2 * pair, 2 * pair + 1)
                 ]
                 spread.append(jnp.concatenate(terms, axis=0))
-        acc[:rows] += lax.dot_general(
+        acc[low : low + rows] += lax.dot_general(
             jnp.concatenate(row_hot, axis=1),
             jnp.concatenate(spread, axis=1),
             (((1,), (1,)), ((), ())),
@@ -193,7 +203,7 @@
         ).start()
 
         def one(i, carry):
-            to_y = (gy + i) % N_GY
+            to_y = (gy + far_first(i, N_GY)) % N_GY
             pltpu.make_async_remote_copy(
                 src_ref=sources.at[slot_of(to_y)],
                 dst_ref=target.at[gy],
@@ -204,13 +214,13 @@
             ).start()
             return carry
 
-        lax.fori_loop(1, N_GY, one, 0)
+        lax.fori_loop(0, N_GY - 1, one, 0)
 
     def scatter_fields(u):
         parts = granules(UNITS[u])
         for i in range(N_GY):
             for g in range(parts):
-                start = (i * parts + g) * GRANULE
+                start = UNITS[u][1] + (i * parts + g) * GRANULE
                 fields[u][i, g] = acc[start : start + GRANULE].astype(jnp.bfloat16)
         to_peers(fields[u], gathered[u], lambda device: device, 0, u)
 
@@ -230,30 +240,38 @@
                     partials[u][r, g, 1, :, lanes] = im.astype(jnp.bfloat16)
         to_peers(partials[u], outs[u], frequency_slot, 1, u)
 
-    def run(u, first, last, phases):
+    def run(pair, low, rows, first, last, phases, arriving=False):
         def step(i, carry):
-            if u == 0:
+            if arriving:
                 arrived = recv.at[pl.ds(0, N_GY)]
                 pltpu.make_async_copy(arrived, arrived, route_recv.at[i]).wait()
-            deposit(UNITS[u], i * phases, phases)
+            deposit(pair, low, rows, i * phases, phases)
             return carry
 
         lax.fori_loop(first // phases, last // phases, step, 0)
 
-    for u in range(count):
-        acc[...] = jnp.zeros_like(acc)
-        if u == 0:
-            run(u, 0, N_GX, 1)
-        elif u == 2:
-            run(u, 0, N_GX, 2)
-        else:
-            run(u, 0, N_GX // 2, 2)
-            transform(u - 1)
-            run(u, N_GX // 2, N_GX, 2)
-        scatter_fields(u)
-        if u == 2:
-            transform(u - 1)
-    transform(count - 1)
+    acc[...] = jnp.zeros_like(acc)
+    run(0, 0, ROWS, 0, 2, 1, arriving=True)
+    run(0, 0, HALF, 2, N_GX, 1, arriving=True)
+    scatter_fields(0)
+    run(0, HALF, HALF, 2, N_GX, 2)
+    scatter_fields(1)
+    transform(0)
+    acc[...] = jnp.zeros_like(acc)
+    run(1, 0, ROWS, 0, N_GX // 2, 2)
+    transform(1)
+    run(1, 0, ROWS, N_GX // 2, N_GX, 2)
+    scatter_fields(2)
+    acc[...] = jnp.zeros_like(acc)
+    run(2, 0, HALF, 0, N_GX, 2)
+    scatter_fields(3)
+    transform(2)
+    run(2, HALF, HALF, 0, N_GX - 2, 2)
+    transform(3)
+    run(2, HALF, HALF, N_GX - 2, N_GX, 2)
+    scatter_fields(4)
+    transform(4)
+    matrix_load.wait()
 
     sent = send_ref.at[pl.ds(0, DEVICES - 1)]
     pltpu.make_async_copy(sent, sent, route_send).wait()
@@ -265,23 +283,12 @@
         pltpu.make_async_copy(outs[u], outs[u], recvs.at[1, u]).wait()
 
 
-def lines_kernel(table_ref, *refs):
-    count = len(UNITS)
-    parts, refs = refs[:count], refs[count:]
-    out_ref, refs = refs[0], refs[1:]
-    held, refs = refs[:count], refs[count:]
-    matrix, staged, load_sems, store_sem = refs
-    freq = reversed4(lax.axis_index("gy"))
-    loads = [pltpu.make_async_copy(table_ref.at[freq], matrix, load_sems.at[count])]
-    loads += [pltpu.make_async_copy(parts[u], held[u], load_sems.at[u]) for u in range(count)]
-    for load in loads:
-        load.start()
-    loads[0].wait()
+def lines_kernel(matrix, *refs):
+    parts, (out_ref, staged, store_sem) = refs[: len(UNITS)], refs[len(UNITS) :]
     for u, (pair, low, rows) in enumerate(UNITS):
-        loads[1 + u].wait()
         sources = N_GY * CY // rows
         for x in range(rows // CY):
-            values = held[u][sources * x : sources * x + sources].reshape(2 * CY, LANES)
+            values = parts[u][sources * x : sources * x + sources].reshape(2 * CY, LANES)
             lines = jnp.dot(matrix[0], values, preferred_element_type=jnp.float32)
             lines += jnp.dot(matrix[1], values, preferred_element_type=jnp.float32)
             to_x = low // CY + x
@@ -318,11 +325,12 @@
     unit_shapes = [(N_GY, granules(unit), GRANULE, LANES) for unit in UNITS]
     half_shapes = [(9, granules(unit), 2, GRANULE, LANES) for unit in UNITS]
     out_shapes = [(N_GY, granules(unit), 2, GRANULE, LANES) for unit in UNITS]
-    parts = pl.pallas_call(
+    *parts, matrix = pl.pallas_call(
         exchange_kernel,
-        out_shape=[jax.ShapeDtypeStruct(shape, jnp.bfloat16) for shape in out_shapes],
-        in_specs=[ANY] * 4,
-        out_specs=[ANY] * len(UNITS),
+        out_shape=[jax.ShapeDtypeStruct(shape, jnp.bfloat16) for shape in out_shapes]
+        + [jax.ShapeDtypeStruct((2, 2 * CY, 2 * CY), jnp.bfloat16)],
+        in_specs=[HBM] * 5,
+        out_specs=[ANY] * (1 + len(UNITS)),
         scratch_shapes=[
             *[pltpu.VMEM(shape, jnp.bfloat16) for shape in unit_shapes],
             *[pltpu.VMEM(shape, jnp.bfloat16) for shape in unit_shapes],
@@ -335,36 +343,40 @@
             pltpu.VMEM((DEVICES, CAP, 8, BP), jnp.bfloat16),
             pltpu.VMEM((DEVICES, CAP, 8, BP), jnp.bfloat16),
             pltpu.VMEM((ROWS, LANES), jnp.float32),
-            pltpu.SemaphoreType.DMA((4,)),
+            pltpu.SemaphoreType.DMA((5,)),
             pltpu.SemaphoreType.DMA,
             pltpu.SemaphoreType.DMA((N_GX,)),
             pltpu.SemaphoreType.DMA((2, len(UNITS))),
             pltpu.SemaphoreType.DMA((2, len(UNITS))),
         ],
         compiler_params=pltpu.CompilerParams(
-            has_side_effects=True, collective_id=0, vmem_limit_bytes=60 << 20
+            has_side_effects=True, collective_id=0, vmem_limit_bytes=28 << 20
         ),
         name="exchange",
     )(
-        owners.reshape(1, NB),
-        jnp.transpose(offsets.reshape(3, NB, BP), (1, 0, 2)),
-        weights.reshape(NB, BP),
-        cells.reshape(NB, BP),
+        *[
+            pltpu.with_memory_space_constraint(array, pltpu.HBM)
+            for array in (
+                owners.reshape(1, NB),
+                jnp.transpose(offsets.reshape(3, NB, BP), (1, 0, 2)),
+                weights.reshape(NB, BP),
+                cells.reshape(NB, BP),
+                table,
+            )
+        ]
     )
     return pl.pallas_call(
         lines_kernel,
         out_shape=jax.ShapeDtypeStruct((2, 6, CX, CY, NZ), jnp.float32),
-        in_specs=[ANY] * (1 + len(UNITS)),
-        out_specs=ANY,
+        in_specs=[VMEM] * (1 + len(UNITS)),
+        out_specs=HBM,
         scratch_shapes=[
-            *[pltpu.VMEM(shape, jnp.bfloat16) for shape in out_shapes],
-            pltpu.VMEM((2, 2 * CY, 2 * CY), jnp.bfloat16),
             pltpu.VMEM((2, 6, CX, CY, NZ), jnp.float32),
-            pltpu.SemaphoreType.DMA((1 + len(UNITS),)),
             pltpu.SemaphoreType.DMA,
         ],
+        compiler_params=pltpu.CompilerParams(vmem_limit_bytes=8 << 20),
         name="lines",
-    )(table, *parts)
+    )(matrix, *parts)
 
 
 def solution(mesh):

time: 66.2 us -> 70.7 us (1.068)
  Pallas kernels: 66.1 us -> 70.6 us
    pallas_call x1, Pallas kernels: 62.8 us -> 68.7 us  [shards(): pl.pallas_call(exchange_kernel, out_shape=[jax.ShapeDtypeStruct(shape, jn...]
    pallas_call x1, Pallas kernels: 3.36 us -> 1.94 us  [shards(): pl.pallas_call(lines_kernel, out_shape=jax.ShapeDtypeStruct((2, 6, CX, CY...]
where the time goes in v3:
time: 70.7 us; the launch traced here: 70.6 us
  Pallas kernels  70.6 us (100%)
    pallas_call x1, Pallas kernels, shards(): pl.pallas_call(exchange_kernel, out_shape=[jax.ShapeDtypeStruct(shape, jn...  68.7 us
    pallas_call x1, Pallas kernels, shards(): pl.pallas_call(lines_kernel, out_shape=jax.ShapeDtypeStruct((2, 6, CX, CY...  1.94 us

profile of v3, /device:TPU:0, one launch (start us, length us, event | category | flops | bytes accessed | tf_op | source)
XLA Modules:
  0.0 70.6 jit_solution(16699328129113941224)
XLA Ops:
  0.0 68.7 %exchange.1 = (bf16[16,1,2,16,256]{4,3,2,1,0:T(8,128)(2,1)S(1)}, bf16[16,1,2,16,256]{4,3,2,1,0:T(8,128)(2,1)S(1)}, bf16[16,2,2,16,256]{4,3,2,1,0:T(8,128)(2,1)S(...) custom-call(s32[1,128]{1,0:T(1,128)} %bitcast.9, ...), custom_call_target="tpu_custom_call" | custom-call | tf_op jit(solution)/shard_map/exchange/pallas_call | solution.py:328
  68.7 1.9 %lines.1 = f32[2,6,8,64,128]{4,3,2,1,0:T(8,128)} custom-call(bf16[2,128,128]{2,1,0:T(8,128)(2,1)S(1)} %get-tuple-element.11.matrix, bf16[16,1,2,16,256]{4,3,2,1,0:T(8,128)(2,1)S(1)} %get-tuple-element.12.refs_0_, bf16[16,1,2,16,256]{4,3,2,1,0:T(8,128)(2,1)S(1)} %get-tuple-element.13.refs_1_, bf16[16,2,2,16,256]{4,3,2,1,0:T(8,128)(2,1)S(1)} %get-tuple-element.14.refs_2_, ...), custom_call_target="tpu_custom_call" | custom-call | tf_op jit(solution)/shard_map/lines/pallas_call | solution.py:368

commit v4 on v3

--- a/solution.py
+++ b/solution.py
@@ -22,7 +22,7 @@
 LANES = 2 * NZ
 GRANULE = 16
 HALF = ROWS // 2
-UNITS = ((0, 0, HALF), (0, HALF, HALF), (1, 0, ROWS), (2, 0, HALF), (2, HALF, HALF))
+UNITS = ((0, 0, ROWS), (1, 0, HALF), (1, HALF, HALF), (2, 0, HALF), (2, HALF, HALF))
 MESH = pl.DeviceIdType.MESH
 ANY = pl.BlockSpec(memory_space=pl.ANY)
 HBM = pl.BlockSpec(memory_space=pltpu.HBM)
@@ -31,10 +31,6 @@
 
 def granules(unit):
     return unit[2] // (N_GY * GRANULE)
-
-
-def far_first(k, count):
-    return count // 2 + (1 - 2 * (k % 2)) * ((k + 1) // 2)
 
 
 def reversed4(value):
@@ -130,13 +126,17 @@
     matrix_load.start()
     barrier = pltpu.get_barrier_semaphore()
 
-    def greet(i, carry):
-        to_x = (gx + far_first(i // N_GY, N_GX)) % N_GX
-        to_y = (gy + far_first(i % N_GY, N_GY)) % N_GY
-        pl.semaphore_signal(barrier, inc=1, device_id=(to_x, to_y), device_id_type=MESH)
+    peers_y = [gy] + [lax.rem(gy + i, N_GY) for i in range(1, N_GY)]
+
+    def greet(j, carry):
+        to_x = lax.rem(gx + j, N_GX)
+        for to_y in peers_y:
+            pl.semaphore_signal(barrier, inc=1, device_id=(to_x, to_y), device_id_type=MESH)
         return carry
 
-    lax.fori_loop(0, DEVICES - 1, greet, 0)
+    for to_y in peers_y[1:]:
+        pl.semaphore_signal(barrier, inc=1, device_id=(gx, to_y), device_id_type=MESH)
+    lax.fori_loop(1, N_GX, greet, 0)
     for load in loads:
         load.wait()
     write_slots(owner_ref[...], offset_ref, weight_ref[...], cell_ref[...], planes, send_ref)
@@ -144,11 +144,8 @@
 
     pltpu.make_async_copy(send_ref.at[me], recv.at[me], route_recv.at[0]).start()
 
-    def route(j, last):
-        to_x = (gx + j) % N_GX
-
-        def one(i, carry):
-            to_y = (gy + far_first(i, N_GY)) % N_GY
+    def route(j, to_x, peers):
+        for to_y in peers:
             pltpu.make_async_remote_copy(
                 src_ref=send_ref.at[to_x * N_GY + to_y],
                 dst_ref=recv.at[me],
@@ -157,17 +154,13 @@
                 device_id=(to_x, to_y),
                 device_id_type=MESH,
             ).start()
-            return carry
-
-        lax.fori_loop(0, last, one, 0)
-
-    route(0, N_GY - 1)
-
-    def route_all(j, carry):
-        route(j, N_GY)
+
+    def route_step(j, carry):
+        route(j, lax.rem(gx + j, N_GX), peers_y)
         return carry
 
-    lax.fori_loop(1, N_GX, route_all, 0)
+    route(0, gx, peers_y[1:])
+    lax.fori_loop(1, N_GX, route_step, 0)
 
     depth_index = lax.broadcasted_iota(jnp.int32, (NZ, BP), 0)
     depth_index = depth_index.astype(jnp.float32).astype(jnp.bfloat16)
@@ -179,7 +172,7 @@
         row_index = row_index.astype(jnp.float32).astype(jnp.bfloat16)
         row_hot, spread = [], []
         for phase in range(phases):
-            base = (gx + N_GX - (first + phase)) % N_GX * N_GY
+            base = lax.rem(gx + N_GX - (first + phase), N_GX) * N_GY
             for slot in range(N_GY * CAP):
                 block = recv[base + slot // CAP, slot % CAP]
                 row = jnp.broadcast_to(block[6:7], (rows, BP))
@@ -202,8 +195,7 @@
             sources.at[slot_of(gy)], target.at[gy], recvs.at[stage, unit_index]
         ).start()
 
-        def one(i, carry):
-            to_y = (gy + far_first(i, N_GY)) % N_GY
+        for to_y in peers_y[1:]:
             pltpu.make_async_remote_copy(
                 src_ref=sources.at[slot_of(to_y)],
                 dst_ref=target.at[gy],
@@ -212,9 +204,6 @@
                 device_id=(gx, to_y),
                 device_id_type=MESH,
             ).start()
-            return carry
-
-        lax.fori_loop(0, N_GY - 1, one, 0)
 
     def scatter_fields(u):
         parts = granules(UNITS[u])
@@ -225,8 +214,10 @@
         to_peers(fields[u], gathered[u], lambda device: device, 0, u)
 
     def frequency_slot(device):
-        freq = reversed4(device)
-        return 8 - (freq - 8) * (2 * (freq // 8) - 1)
+        rem, div = lax.rem, lax.div
+        freq = rem(device, 2) * 8 + rem(div(device, 2), 2) * 4
+        freq = freq + rem(div(device, 4), 2) * 2 + div(device, 8)
+        return 8 - (freq - 8) * (2 * div(freq, 8) - 1)
 
     def transform(u):
         pltpu.make_async_copy(gathered[u], gathered[u], recvs.at[0, u]).wait()
@@ -242,9 +233,10 @@
 
     def run(pair, low, rows, first, last, phases, arriving=False):
         def step(i, carry):
-            if arriving:
+            for phase in range(phases if arriving else 0):
                 arrived = recv.at[pl.ds(0, N_GY)]
-                pltpu.make_async_copy(arrived, arrived, route_recv.at[i]).wait()
+                sem = route_recv.at[i * phases + phase]
+                pltpu.make_async_copy(arrived, arrived, sem).wait()
             deposit(pair, low, rows, i * phases, phases)
             return carry
 
@@ -252,24 +244,24 @@
 
     acc[...] = jnp.zeros_like(acc)
     run(0, 0, ROWS, 0, 2, 1, arriving=True)
-    run(0, 0, HALF, 2, N_GX, 1, arriving=True)
+    run(0, 0, ROWS, 2, N_GX, 2, arriving=True)
     scatter_fields(0)
-    run(0, HALF, HALF, 2, N_GX, 2)
+    acc[...] = jnp.zeros_like(acc)
+    run(1, 0, HALF, 0, N_GX, 4)
     scatter_fields(1)
+    run(1, HALF, HALF, 0, N_GX // 2, 2)
     transform(0)
+    run(1, HALF, HALF, N_GX // 2, N_GX, 2)
+    scatter_fields(2)
+    transform(1)
     acc[...] = jnp.zeros_like(acc)
-    run(1, 0, ROWS, 0, N_GX // 2, 2)
-    transform(1)
-    run(1, 0, ROWS, N_GX // 2, N_GX, 2)
-    scatter_fields(2)
-    acc[...] = jnp.zeros_like(acc)
-    run(2, 0, HALF, 0, N_GX, 2)
+    run(2, 0, HALF, 0, N_GX, 4)
     scatter_fields(3)
+    run(2, HALF, HALF, 0, N_GX - 2, 2)
     transform(2)
-    run(2, HALF, HALF, 0, N_GX - 2, 2)
-    transform(3)
     run(2, HALF, HALF, N_GX - 2, N_GX, 2)
     scatter_fields(4)
+    transform(3)
     transform(4)
     matrix_load.wait()
 
@@ -350,7 +342,7 @@
             pltpu.SemaphoreType.DMA((2, len(UNITS))),
         ],
         compiler_params=pltpu.CompilerParams(
-            has_side_effects=True, collective_id=0, vmem_limit_bytes=28 << 20
+            has_side_effects=True, collective_id=0, vmem_limit_bytes=48 << 20
         ),
         name="exchange",
     )(

time: 70.7 us -> 60.1 us (0.85)
  Pallas kernels: 70.6 us -> 60 us
    pallas_call x1, Pallas kernels: 68.7 us -> 58 us  [shards(): pl.pallas_call(exchange_kernel, out_shape=[jax.ShapeDtypeStruct(shape, jn...]
where the time goes in v4:
time: 60.1 us; the launch traced here: 60 us
  Pallas kernels  60 us (100%)
    pallas_call x1, Pallas kernels, shards(): pl.pallas_call(exchange_kernel, out_shape=[jax.ShapeDtypeStruct(shape, jn...  58 us
    pallas_call x1, Pallas kernels, shards(): pl.pallas_call(lines_kernel, out_shape=jax.ShapeDtypeStruct((2, 6, CX, CY...  1.94 us

profile of v4, /device:TPU:0, one launch (start us, length us, event | category | flops | bytes accessed | tf_op | source)
XLA Modules:
  0.0 60.0 jit_solution(4314434697211978471)
XLA Ops:
  0.0 58.0 %exchange.1 = (bf16[16,2,2,16,256]{4,3,2,1,0:T(8,128)(2,1)S(1)}, bf16[16,1,2,16,256]{4,3,2,1,0:T(8,128)(2,1)S(1)}, bf16[16,1,2,16,256]{4,3,2,1,0:T(8,128)(2,1)S(...) custom-call(s32[1,128]{1,0:T(1,128)} %bitcast.9, ...), custom_call_target="tpu_custom_call" | custom-call | tf_op jit(solution)/shard_map/exchange/pallas_call | solution.py:320
  58.0 1.9 %lines.1 = f32[2,6,8,64,128]{4,3,2,1,0:T(8,128)} custom-call(bf16[2,128,128]{2,1,0:T(8,128)(2,1)S(1)} %get-tuple-element.11.matrix, bf16[16,2,2,16,256]{4,3,2,1,0:T(8,128)(2,1)S(1)} %get-tuple-element.12.refs_0_, bf16[16,1,2,16,256]{4,3,2,1,0:T(8,128)(2,1)S(1)} %get-tuple-element.13.refs_1_, bf16[16,1,2,16,256]{4,3,2,1,0:T(8,128)(2,1)S(1)} %get-tuple-element.14.refs_2_, ...), custom_call_target="tpu_custom_call" | custom-call | tf_op jit(solution)/shard_map/lines/pallas_call | solution.py:360

commit v5 on v4

--- a/solution.py
+++ b/solution.py
@@ -33,6 +33,21 @@
     return unit[2] // (N_GY * GRANULE)
 
 
+def hops(offset):
+    return sum(min(step, 4 - step) for step in offset)
+
+
+def offsets_by_distance(with_z):
+    span = range(4) if with_z else range(1)
+    cores = range(2) if with_z else range(1)
+    every = [(z, c, y, x) for z in span for c in cores for y in range(4) for x in range(4)]
+    return sorted(every, key=lambda o: (hops((o[0], o[2], o[3])), o[1]))
+
+
+ROUTE = offsets_by_distance(True)
+PLANE = offsets_by_distance(False)
+
+
 def reversed4(value):
     return value % 2 * 8 + value // 2 % 2 * 4 + value // 4 % 2 * 2 + value // 8
 
@@ -94,15 +109,28 @@
     send_ref[...] = planes[...].reshape(DEVICES, CAP, 8, BP).astype(jnp.bfloat16)
 
 
+def unit_lines(unit, matrix, part, target, first_k, first_x):
+    sources = N_GY * CY // unit[2]
+    for x in range(unit[2] // CY):
+        values = part[sources * x : sources * x + sources].reshape(2 * CY, LANES)
+        lines = jnp.dot(matrix[0], values, preferred_element_type=jnp.float32)
+        lines += jnp.dot(matrix[1], values, preferred_element_type=jnp.float32)
+        for half in range(2):
+            for k in range(2):
+                target[half, first_k + k, first_x + x] = lines[
+                    half * CY : half * CY + CY, k * NZ : k * NZ + NZ
+                ]
+
+
 def exchange_kernel(owner_hbm, offset_hbm, weight_hbm, cell_hbm, table_hbm, *refs):
     count = len(UNITS)
-    outs, refs = refs[:count], refs[count:]
-    matrix_ref, refs = refs[0], refs[1:]
+    (last_ref, matrix_ref, done_ref), refs = refs[:3], refs[3:]
+    outs, refs = (*refs[: count - 1], last_ref), refs[count - 1 :]
     fields, refs = refs[:count], refs[count:]
     gathered, refs = refs[:count], refs[count:]
     partials, refs = refs[:count], refs[count:]
     owner_ref, offset_ref, weight_ref, cell_ref, planes, send_ref, recv, acc = refs[:8]
-    load_sems, route_send, route_recv, sends, recvs = refs[8:]
+    matrix, staged, load_sems, route_send, route_recv, sends, recvs, done_sems = refs[8:]
     gx = lax.axis_index("gx")
     gy = lax.axis_index("gy")
     me = gx * N_GY + gy
@@ -124,43 +152,37 @@
         table_hbm.at[reversed4(gy)], matrix_ref, load_sems.at[len(loads)]
     )
     matrix_load.start()
+    own_load = pltpu.make_async_copy(table_hbm.at[reversed4(gy)], matrix, load_sems.at[5])
+    own_load.start()
     barrier = pltpu.get_barrier_semaphore()
 
-    peers_y = [gy] + [lax.rem(gy + i, N_GY) for i in range(1, N_GY)]
-
-    def greet(j, carry):
-        to_x = lax.rem(gx + j, N_GX)
-        for to_y in peers_y:
-            pl.semaphore_signal(barrier, inc=1, device_id=(to_x, to_y), device_id_type=MESH)
-        return carry
-
-    for to_y in peers_y[1:]:
-        pl.semaphore_signal(barrier, inc=1, device_id=(gx, to_y), device_id_type=MESH)
-    lax.fori_loop(1, N_GX, greet, 0)
+    rem, div = lax.rem, lax.div
+    columns = {
+        (z, c): rem(div(gx, 2) + z, 4) * 2 + rem(gx + c, 2) for z in range(4) for c in range(2)
+    }
+    places = {
+        (y, x): rem(div(gy, 4) + y, 4) * 4 + rem(gy + x, 4) for y in range(4) for x in range(4)
+    }
+    routes = [(columns[offset[:2]], places[offset[2:]]) for offset in ROUTE]
+    peers = [places[offset[2:]] for offset in PLANE[1:]]
+    for device in routes[:0:-1]:
+        pl.semaphore_signal(barrier, inc=1, device_id=device, device_id_type=MESH)
     for load in loads:
         load.wait()
     write_slots(owner_ref[...], offset_ref, weight_ref[...], cell_ref[...], planes, send_ref)
     pl.semaphore_wait(barrier, DEVICES - 1)
 
-    pltpu.make_async_copy(send_ref.at[me], recv.at[me], route_recv.at[0]).start()
-
-    def route(j, to_x, peers):
-        for to_y in peers:
+    pltpu.make_async_copy(send_ref.at[me], recv.at[0], route_recv.at[0]).start()
+    for i, device in enumerate(routes):
+        if i:
             pltpu.make_async_remote_copy(
-                src_ref=send_ref.at[to_x * N_GY + to_y],
-                dst_ref=recv.at[me],
+                src_ref=send_ref.at[device[0] * N_GY + device[1]],
+                dst_ref=recv.at[i],
                 send_sem=route_send,
-                recv_sem=route_recv.at[j],
-                device_id=(to_x, to_y),
+                recv_sem=route_recv.at[i // N_GY],
+                device_id=device,
                 device_id_type=MESH,
             ).start()
-
-    def route_step(j, carry):
-        route(j, lax.rem(gx + j, N_GX), peers_y)
-        return carry
-
-    route(0, gx, peers_y[1:])
-    lax.fori_loop(1, N_GX, route_step, 0)
 
     depth_index = lax.broadcasted_iota(jnp.int32, (NZ, BP), 0)
     depth_index = depth_index.astype(jnp.float32).astype(jnp.bfloat16)
@@ -172,7 +194,7 @@
         row_index = row_index.astype(jnp.float32).astype(jnp.bfloat16)
         row_hot, spread = [], []
         for phase in range(phases):
-            base = lax.rem(gx + N_GX - (first + phase), N_GX) * N_GY
+            base = (first + phase) * N_GY
             for slot in range(N_GY * CAP):
                 block = recv[base + slot // CAP, slot % CAP]
                 row = jnp.broadcast_to(block[6:7], (rows, BP))
@@ -195,7 +217,7 @@
             sources.at[slot_of(gy)], target.at[gy], recvs.at[stage, unit_index]
         ).start()
 
-        for to_y in peers_y[1:]:
+        for to_y in peers:
             pltpu.make_async_remote_copy(
                 src_ref=sources.at[slot_of(to_y)],
                 dst_ref=target.at[gy],
@@ -214,7 +236,6 @@
         to_peers(fields[u], gathered[u], lambda device: device, 0, u)
 
     def frequency_slot(device):
-        rem, div = lax.rem, lax.div
         freq = rem(device, 2) * 8 + rem(div(device, 2), 2) * 4
         freq = freq + rem(div(device, 4), 2) * 2 + div(device, 8)
         return 8 - (freq - 8) * (2 * div(freq, 8) - 1)
@@ -231,8 +252,14 @@
                     partials[u][r, g, 1, :, lanes] = im.astype(jnp.bfloat16)
         to_peers(partials[u], outs[u], frequency_slot, 1, u)
 
-    def run(pair, low, rows, first, last, phases, arriving=False):
+    def run(pair, low, rows, first, last, phases, arriving=False, between=None):
         def step(i, carry):
+            if between is not None:
+
+                @pl.when(i == between[0])
+                def _():
+                    transform(between[1])
+
             for phase in range(phases if arriving else 0):
                 arrived = recv.at[pl.ds(0, N_GY)]
                 sem = route_recv.at[i * phases + phase]
@@ -249,21 +276,35 @@
     acc[...] = jnp.zeros_like(acc)
     run(1, 0, HALF, 0, N_GX, 4)
     scatter_fields(1)
-    run(1, HALF, HALF, 0, N_GX // 2, 2)
-    transform(0)
-    run(1, HALF, HALF, N_GX // 2, N_GX, 2)
+    run(1, HALF, HALF, 0, N_GX, 2, between=(2, 0))
     scatter_fields(2)
     transform(1)
     acc[...] = jnp.zeros_like(acc)
     run(2, 0, HALF, 0, N_GX, 4)
     scatter_fields(3)
-    run(2, HALF, HALF, 0, N_GX - 2, 2)
     transform(2)
-    run(2, HALF, HALF, N_GX - 2, N_GX, 2)
+    run(2, HALF, HALF, 0, N_GX, 2, between=(3, 3))
     scatter_fields(4)
-    transform(3)
+
+    def finish(u):
+        pltpu.make_async_copy(outs[u], outs[u], recvs.at[1, u]).wait()
+        pair, low, rows = UNITS[u]
+        unit_lines(UNITS[u], matrix, outs[u], staged, 2 * pair, low // CY)
+        for half in range(2):
+            at = (half, pl.ds(2 * pair, 2), pl.ds(low // CY, rows // CY))
+            copy = pltpu.make_async_copy(staged.at[at], done_ref.at[at], done_sems.at[u, half])
+            copy.start()
+            moved.append(copy)
+
+    moved = [matrix_load]
+    own_load.wait()
+    finish(0)
+    finish(1)
     transform(4)
-    matrix_load.wait()
+    finish(2)
+    finish(3)
+    for copy in moved:
+        copy.wait()
 
     sent = send_ref.at[pl.ds(0, DEVICES - 1)]
     pltpu.make_async_copy(sent, sent, route_send).wait()
@@ -272,28 +313,26 @@
         pltpu.make_async_copy(sent, sent, sends.at[0, u]).wait()
         sent = outs[u].at[pl.ds(0, N_GY - 1)]
         pltpu.make_async_copy(sent, sent, sends.at[1, u]).wait()
-        pltpu.make_async_copy(outs[u], outs[u], recvs.at[1, u]).wait()
-
-
-def lines_kernel(matrix, *refs):
-    parts, (out_ref, staged, store_sem) = refs[: len(UNITS)], refs[len(UNITS) :]
-    for u, (pair, low, rows) in enumerate(UNITS):
-        sources = N_GY * CY // rows
-        for x in range(rows // CY):
-            values = parts[u][sources * x : sources * x + sources].reshape(2 * CY, LANES)
-            lines = jnp.dot(matrix[0], values, preferred_element_type=jnp.float32)
-            lines += jnp.dot(matrix[1], values, preferred_element_type=jnp.float32)
-            to_x = low // CY + x
-            for half in range(2):
-                for k in range(2):
-                    staged[half, 2 * pair + k, to_x] = lines[
-                        half * CY : half * CY + CY, k * NZ : k * NZ + NZ
-                    ]
-            if x % 4 == 3:
-                for half in range(2):
-                    at = (half, pl.ds(2 * pair, 2), pl.ds(to_x - 3, 4))
-                    pltpu.make_async_copy(staged.at[at], out_ref.at[at], store_sem).start()
-    pltpu.make_async_copy(staged, out_ref, store_sem).wait()
+    pltpu.make_async_copy(outs[4], outs[4], recvs.at[1, 4]).wait()
+
+
+def lines_kernel(matrix, part, done_ref, out_ref, last, sems):
+    pair, low, rows = UNITS[-1]
+    copies = []
+    for half in range(2):
+        for u in range(len(UNITS) - 1):
+            at = (half, pl.ds(2 * UNITS[u][0], 2), pl.ds(UNITS[u][1] // CY, UNITS[u][2] // CY))
+            copies.append((done_ref.at[at], out_ref.at[at]))
+    for i, (source, target) in enumerate(copies):
+        pltpu.make_async_copy(source, target, sems.at[i]).start()
+    unit_lines(UNITS[-1], matrix, part, last, 0, 0)
+    for half in range(2):
+        at = (half, pl.ds(2 * pair, 2), pl.ds(low // CY, rows // CY))
+        copies.append((last.at[half], out_ref.at[at]))
+        i = len(copies) - 1
+        pltpu.make_async_copy(*copies[i], sems.at[i]).start()
+    for i, (source, target) in enumerate(copies):
+        pltpu.make_async_copy(source, target, sems.at[i]).wait()
 
 
 def line_table():
@@ -317,13 +356,17 @@
     unit_shapes = [(N_GY, granules(unit), GRANULE, LANES) for unit in UNITS]
     half_shapes = [(9, granules(unit), 2, GRANULE, LANES) for unit in UNITS]
     out_shapes = [(N_GY, granules(unit), 2, GRANULE, LANES) for unit in UNITS]
-    *parts, matrix = pl.pallas_call(
+    part, matrix, done = pl.pallas_call(
         exchange_kernel,
-        out_shape=[jax.ShapeDtypeStruct(shape, jnp.bfloat16) for shape in out_shapes]
-        + [jax.ShapeDtypeStruct((2, 2 * CY, 2 * CY), jnp.bfloat16)],
+        out_shape=[
+            jax.ShapeDtypeStruct(out_shapes[-1], jnp.bfloat16),
+            jax.ShapeDtypeStruct((2, 2 * CY, 2 * CY), jnp.bfloat16),
+            jax.ShapeDtypeStruct((2, 6, CX, CY, NZ), jnp.float32),
+        ],
         in_specs=[HBM] * 5,
-        out_specs=[ANY] * (1 + len(UNITS)),
+        out_specs=[ANY] * 3,
         scratch_shapes=[
+            *[pltpu.VMEM(shape, jnp.bfloat16) for shape in out_shapes[:-1]],
             *[pltpu.VMEM(shape, jnp.bfloat16) for shape in unit_shapes],
             *[pltpu.VMEM(shape, jnp.bfloat16) for shape in unit_shapes],
             *[pltpu.VMEM(shape, jnp.bfloat16) for shape in half_shapes],
@@ -335,11 +378,14 @@
             pltpu.VMEM((DEVICES, CAP, 8, BP), jnp.bfloat16),
             pltpu.VMEM((DEVICES, CAP, 8, BP), jnp.bfloat16),
             pltpu.VMEM((ROWS, LANES), jnp.float32),
-            pltpu.SemaphoreType.DMA((5,)),
+            pltpu.VMEM((2, 2 * CY, 2 * CY), jnp.bfloat16),
+            pltpu.VMEM((2, 6, CX, CY, NZ), jnp.float32),
+            pltpu.SemaphoreType.DMA((6,)),
             pltpu.SemaphoreType.DMA,
             pltpu.SemaphoreType.DMA((N_GX,)),
             pltpu.SemaphoreType.DMA((2, len(UNITS))),
             pltpu.SemaphoreType.DMA((2, len(UNITS))),
+            pltpu.SemaphoreType.DMA((len(UNITS) - 1, 2)),
         ],
         compiler_params=pltpu.CompilerParams(
             has_side_effects=True, collective_id=0, vmem_limit_bytes=48 << 20
@@ -360,15 +406,15 @@
     return pl.pallas_call(
         lines_kernel,
         out_shape=jax.ShapeDtypeStruct((2, 6, CX, CY, NZ), jnp.float32),
-        in_specs=[VMEM] * (1 + len(UNITS)),
+        in_specs=[VMEM] * 3,
         out_specs=HBM,
         scratch_shapes=[
-            pltpu.VMEM((2, 6, CX, CY, NZ), jnp.float32),
-            pltpu.SemaphoreType.DMA,
+            pltpu.VMEM((2, 2, UNITS[-1][2] // CY, CY, NZ), jnp.float32),
+            pltpu.SemaphoreType.DMA((2 * len(UNITS),)),
         ],
         compiler_params=pltpu.CompilerParams(vmem_limit_bytes=8 << 20),
         name="lines",
-    )(matrix, *parts)
+    )(matrix, part, done)
 
 
 def solution(mesh):

time: 60.1 us -> 61.1 us (1.017)
  Pallas kernels: 60 us -> 61 us
    pallas_call x1, Pallas kernels: 58 us -> 59.2 us  [shards(): pl.pallas_call(exchange_kernel, out_shape=[jax.ShapeDtypeStruct(out_shape...]
where the time goes in v5:
time: 61.1 us; the launch traced here: 61 us
  Pallas kernels  61 us (100%)
    pallas_call x1, Pallas kernels, shards(): pl.pallas_call(exchange_kernel, out_shape=[jax.ShapeDtypeStruct(out_shape...  59.2 us
    pallas_call x1, Pallas kernels, shards(): pl.pallas_call(lines_kernel, out_shape=jax.ShapeDtypeStruct((2, 6, CX, CY...  1.74 us

profile of v5, /device:TPU:0, one launch (start us, length us, event | category | flops | bytes accessed | tf_op | source)
XLA Modules:
  0.0 61.0 jit_solution(3523615866104761720)
XLA Ops:
  0.0 59.2 %exchange.1 = (bf16[16,1,2,16,256]{4,3,2,1,0:T(8,128)(2,1)S(1)}, bf16[2,128,128]{2,1,0:T(8,128)(2,1)S(1)}, f32[2,6,8,64,128]{4,3,2,1,0:T(8,128)S(1)}) custom-call(s32[1,128]{1,0:T(1,128)} %bitcast.9, f32[128,3,128]{2,1,0:T(4,128)} %bitcast.6, f32[128,128]{1,0:T(8,128)} %bitcast.7, s32[128,128]{1,0:T(8,128)} %bitcast.8, ...), custom_call_target="tpu_custom_call" | custom-call | tf_op jit(solution)/shard_map/exchange/pallas_call | solution.py:359
  59.2 1.7 %lines.1 = f32[2,6,8,64,128]{4,3,2,1,0:T(8,128)} custom-call(bf16[2,128,128]{2,1,0:T(8,128)(2,1)S(1)} %get-tuple-element.8.matrix, bf16[16,1,2,16,256]{4,3,2,1,0:T(8,128)(2,1)S(1)} %get-tuple-element.9.part, f32[2,6,8,64,128]{4,3,2,1,0:T(8,128)S(1)} %get-tuple-element.10.done_ref), custom_call_target="tpu_custom_call" | custom-call | tf_op jit(solution)/shard_map/lines/pallas_call | solution.py:406

commit v6 on v5

--- a/solution.py
+++ b/solution.py
@@ -22,7 +22,7 @@
 LANES = 2 * NZ
 GRANULE = 16
 HALF = ROWS // 2
-UNITS = ((0, 0, ROWS), (1, 0, HALF), (1, HALF, HALF), (2, 0, HALF), (2, HALF, HALF))
+UNITS = tuple((pair, low, HALF) for pair in range(3) for low in (0, HALF))
 MESH = pl.DeviceIdType.MESH
 ANY = pl.BlockSpec(memory_space=pl.ANY)
 HBM = pl.BlockSpec(memory_space=pltpu.HBM)
@@ -270,21 +270,17 @@
         lax.fori_loop(first // phases, last // phases, step, 0)
 
     acc[...] = jnp.zeros_like(acc)
-    run(0, 0, ROWS, 0, 2, 1, arriving=True)
-    run(0, 0, ROWS, 2, N_GX, 2, arriving=True)
+    run(0, 0, ROWS, 0, 4, 1, arriving=True)
+    run(0, 0, HALF, 4, N_GX, 2, arriving=True)
     scatter_fields(0)
-    acc[...] = jnp.zeros_like(acc)
-    run(1, 0, HALF, 0, N_GX, 4)
+    run(0, HALF, HALF, 4, N_GX, 2)
     scatter_fields(1)
-    run(1, HALF, HALF, 0, N_GX, 2, between=(2, 0))
-    scatter_fields(2)
-    transform(1)
-    acc[...] = jnp.zeros_like(acc)
-    run(2, 0, HALF, 0, N_GX, 4)
-    scatter_fields(3)
-    transform(2)
-    run(2, HALF, HALF, 0, N_GX, 2, between=(3, 3))
-    scatter_fields(4)
+    for u in range(2, count):
+        if u % 2 == 0:
+            acc[...] = jnp.zeros_like(acc)
+        run(*UNITS[u], 0, N_GX, 4, between=(1, 0) if u == 2 else None)
+        scatter_fields(u)
+        transform(u - 1)
 
     def finish(u):
         pltpu.make_async_copy(outs[u], outs[u], recvs.at[1, u]).wait()
@@ -298,11 +294,10 @@
 
     moved = [matrix_load]
     own_load.wait()
-    finish(0)
-    finish(1)
-    transform(4)
-    finish(2)
-    finish(3)
+    for u in range(count - 2):
+        finish(u)
+    transform(count - 1)
+    finish(count - 2)
     for copy in moved:
         copy.wait()
 
@@ -313,7 +308,7 @@
         pltpu.make_async_copy(sent, sent, sends.at[0, u]).wait()
         sent = outs[u].at[pl.ds(0, N_GY - 1)]
         pltpu.make_async_copy(sent, sent, sends.at[1, u]).wait()
-    pltpu.make_async_copy(outs[4], outs[4], recvs.at[1, 4]).wait()
+    pltpu.make_async_copy(outs[-1], outs[-1], recvs.at[1, count - 1]).wait()
 
 
 def lines_kernel(matrix, part, done_ref, out_ref, last, sems):

time: 61.1 us -> 59.4 us (0.972)
  Pallas kernels: 61 us -> 59.1 us
    pallas_call x1, Pallas kernels: 59.2 us -> 57.4 us  [shards(): pl.pallas_call(exchange_kernel, out_shape=[jax.ShapeDtypeStruct(out_shape...]
where the time goes in v6:
time: 59.4 us; the launch traced here: 59.3 us
  Pallas kernels  59.1 us (99%)
    pallas_call x1, Pallas kernels, shards(): pl.pallas_call(exchange_kernel, out_shape=[jax.ShapeDtypeStruct(out_shape...  57.4 us
    pallas_call x1, Pallas kernels, shards(): pl.pallas_call(lines_kernel, out_shape=jax.ShapeDtypeStruct((2, 6, CX, CY...  1.76 us

profile of v6, /device:TPU:0, one launch (start us, length us, event | category | flops | bytes accessed | tf_op | source)
XLA Modules:
  0.0 59.3 jit_solution(14215024883620661634)
XLA Ops:
  0.0 57.4 %exchange.1 = (bf16[16,1,2,16,256]{4,3,2,1,0:T(8,128)(2,1)S(1)}, bf16[2,128,128]{2,1,0:T(8,128)(2,1)S(1)}, f32[2,6,8,64,128]{4,3,2,1,0:T(8,128)S(1)}) custom-call(s32[1,128]{1,0:T(1,128)} %bitcast.9, f32[128,3,128]{2,1,0:T(4,128)} %bitcast.6, f32[128,128]{1,0:T(8,128)} %bitcast.7, s32[128,128]{1,0:T(8,128)} %bitcast.8, ...), custom_call_target="tpu_custom_call" | custom-call | tf_op jit(solution)/shard_map/exchange/pallas_call | solution.py:354
  57.4 1.8 %lines.1 = f32[2,6,8,64,128]{4,3,2,1,0:T(8,128)} custom-call(bf16[2,128,128]{2,1,0:T(8,128)(2,1)S(1)} %get-tuple-element.8.matrix, bf16[16,1,2,16,256]{4,3,2,1,0:T(8,128)(2,1)S(1)} %get-tuple-element.9.part, f32[2,6,8,64,128]{4,3,2,1,0:T(8,128)S(1)} %get-tuple-element.10.done_ref), custom_call_target="tpu_custom_call" | custom-call | tf_op jit(solution)/shard_map/lines/pallas_call | solution.py:401

commit v7 on v6

--- a/solution.py
+++ b/solution.py
@@ -146,14 +146,6 @@
             )
         )
     ]
-    for load in loads:
-        load.start()
-    matrix_load = pltpu.make_async_copy(
-        table_hbm.at[reversed4(gy)], matrix_ref, load_sems.at[len(loads)]
-    )
-    matrix_load.start()
-    own_load = pltpu.make_async_copy(table_hbm.at[reversed4(gy)], matrix, load_sems.at[5])
-    own_load.start()
     barrier = pltpu.get_barrier_semaphore()
 
     rem, div = lax.rem, lax.div
@@ -167,6 +159,14 @@
     peers = [places[offset[2:]] for offset in PLANE[1:]]
     for device in routes[:0:-1]:
         pl.semaphore_signal(barrier, inc=1, device_id=device, device_id_type=MESH)
+    for load in loads:
+        load.start()
+    matrix_load = pltpu.make_async_copy(
+        table_hbm.at[reversed4(gy)], matrix_ref, load_sems.at[len(loads)]
+    )
+    matrix_load.start()
+    own_load = pltpu.make_async_copy(table_hbm.at[reversed4(gy)], matrix, load_sems.at[5])
+    own_load.start()
     for load in loads:
         load.wait()
     write_slots(owner_ref[...], offset_ref, weight_ref[...], cell_ref[...], planes, send_ref)
@@ -271,7 +271,7 @@
 
     acc[...] = jnp.zeros_like(acc)
     run(0, 0, ROWS, 0, 4, 1, arriving=True)
-    run(0, 0, HALF, 4, N_GX, 2, arriving=True)
+    run(0, 0, HALF, 4, N_GX, 1, arriving=True)
     scatter_fields(0)
     run(0, HALF, HALF, 4, N_GX, 2)
     scatter_fields(1)
@@ -294,9 +294,10 @@
 
     moved = [matrix_load]
     own_load.wait()
-    for u in range(count - 2):
+    for u in range(count - 3):
         finish(u)
     transform(count - 1)
+    finish(count - 3)
     finish(count - 2)
     for copy in moved:
         copy.wait()

time: 59.4 us -> 59 us (level)
  no operation moved by 1% of the time
where the time goes in v7:
time: 59 us; the launch traced here: 58.9 us
  Pallas kernels  58.9 us (100%)
    pallas_call x1, Pallas kernels, shards(): pl.pallas_call(exchange_kernel, out_shape=[jax.ShapeDtypeStruct(out_shape...  57.1 us
    pallas_call x1, Pallas kernels, shards(): pl.pallas_call(lines_kernel, out_shape=jax.ShapeDtypeStruct((2, 6, CX, CY...  1.76 us

profile of v7, /device:TPU:0, one launch (start us, length us, event | category | flops | bytes accessed | tf_op | source)
XLA Modules:
  0.0 58.9 jit_solution(7790205593621211561)
XLA Ops:
  0.0 57.1 %exchange.1 = (bf16[16,1,2,16,256]{4,3,2,1,0:T(8,128)(2,1)S(1)}, bf16[2,128,128]{2,1,0:T(8,128)(2,1)S(1)}, f32[2,6,8,64,128]{4,3,2,1,0:T(8,128)S(1)}) custom-call(s32[1,128]{1,0:T(1,128)} %bitcast.9, f32[128,3,128]{2,1,0:T(4,128)} %bitcast.6, f32[128,128]{1,0:T(8,128)} %bitcast.7, s32[128,128]{1,0:T(8,128)} %bitcast.8, ...), custom_call_target="tpu_custom_call" | custom-call | tf_op jit(solution)/shard_map/exchange/pallas_call | solution.py:355
  57.1 1.8 %lines.1 = f32[2,6,8,64,128]{4,3,2,1,0:T(8,128)} custom-call(bf16[2,128,128]{2,1,0:T(8,128)(2,1)S(1)} %get-tuple-element.8.matrix, bf16[16,1,2,16,256]{4,3,2,1,0:T(8,128)(2,1)S(1)} %get-tuple-element.9.part, f32[2,6,8,64,128]{4,3,2,1,0:T(8,128)S(1)} %get-tuple-element.10.done_ref), custom_call_target="tpu_custom_call" | custom-call | tf_op jit(solution)/shard_map/lines/pallas_call | solution.py:402

commit v8 on v7

--- a/solution.py
+++ b/solution.py
@@ -270,10 +270,10 @@
         lax.fori_loop(first // phases, last // phases, step, 0)
 
     acc[...] = jnp.zeros_like(acc)
-    run(0, 0, ROWS, 0, 4, 1, arriving=True)
-    run(0, 0, HALF, 4, N_GX, 1, arriving=True)
+    run(0, 0, ROWS, 0, 3, 1, arriving=True)
+    run(0, 0, HALF, 3, N_GX, 1, arriving=True)
     scatter_fields(0)
-    run(0, HALF, HALF, 4, N_GX, 2)
+    run(0, HALF, HALF, 3, N_GX, 1)
     scatter_fields(1)
     for u in range(2, count):
         if u % 2 == 0:

time: 59 us -> 59.7 us (1.012)
  Pallas kernels: 58.9 us -> 59.6 us
    pallas_call x1, Pallas kernels: 57.1 us -> 57.8 us  [shards(): pl.pallas_call(exchange_kernel, out_shape=[jax.ShapeDtypeStruct(out_shape...]
where the time goes in v8:
time: 59.7 us; the launch traced here: 59.6 us
  Pallas kernels  59.6 us (100%)
    pallas_call x1, Pallas kernels, shards(): pl.pallas_call(exchange_kernel, out_shape=[jax.ShapeDtypeStruct(out_shape...  57.8 us
    pallas_call x1, Pallas kernels, shards(): pl.pallas_call(lines_kernel, out_shape=jax.ShapeDtypeStruct((2, 6, CX, CY...  1.76 us

profile of v8, /device:TPU:0, one launch (start us, length us, event | category | flops | bytes accessed | tf_op | source)
XLA Modules:
  0.0 59.6 jit_solution(823296203197798947)
XLA Ops:
  0.0 57.8 %exchange.1 = (bf16[16,1,2,16,256]{4,3,2,1,0:T(8,128)(2,1)S(1)}, bf16[2,128,128]{2,1,0:T(8,128)(2,1)S(1)}, f32[2,6,8,64,128]{4,3,2,1,0:T(8,128)S(1)}) custom-call(s32[1,128]{1,0:T(1,128)} %bitcast.9, f32[128,3,128]{2,1,0:T(4,128)} %bitcast.6, f32[128,128]{1,0:T(8,128)} %bitcast.7, s32[128,128]{1,0:T(8,128)} %bitcast.8, ...), custom_call_target="tpu_custom_call" | custom-call | tf_op jit(solution)/shard_map/exchange/pallas_call | solution.py:355
  57.9 1.8 %lines.1 = f32[2,6,8,64,128]{4,3,2,1,0:T(8,128)} custom-call(bf16[2,128,128]{2,1,0:T(8,128)(2,1)S(1)} %get-tuple-element.8.matrix, bf16[16,1,2,16,256]{4,3,2,1,0:T(8,128)(2,1)S(1)} %get-tuple-element.9.part, f32[2,6,8,64,128]{4,3,2,1,0:T(8,128)S(1)} %get-tuple-element.10.done_ref), custom_call_target="tpu_custom_call" | custom-call | tf_op jit(solution)/shard_map/lines/pallas_call | solution.py:402

commit v9 on v7

--- a/solution.py
+++ b/solution.py
@@ -217,7 +217,8 @@
             sources.at[slot_of(gy)], target.at[gy], recvs.at[stage, unit_index]
         ).start()
 
-        for to_y in peers:
+        ending = stage == 1 and unit_index == count - 1
+        for to_y in peers[::-1] if ending else peers:
             pltpu.make_async_remote_copy(
                 src_ref=sources.at[slot_of(to_y)],
                 dst_ref=target.at[gy],

time: 59 us -> 58.7 us (level)
  no operation moved by 1% of the time
where the time goes in v9:
time: 58.7 us; the launch traced here: 58.6 us
  Pallas kernels  58.6 us (100%)
    pallas_call x1, Pallas kernels, shards(): pl.pallas_call(exchange_kernel, out_shape=[jax.ShapeDtypeStruct(out_shape...  56.8 us
    pallas_call x1, Pallas kernels, shards(): pl.pallas_call(lines_kernel, out_shape=jax.ShapeDtypeStruct((2, 6, CX, CY...  1.76 us

profile of v9, /device:TPU:0, one launch (start us, length us, event | category | flops | bytes accessed | tf_op | source)
XLA Modules:
  0.0 58.6 jit_solution(14148176732737887226)
XLA Ops:
  0.0 56.8 %exchange.1 = (bf16[16,1,2,16,256]{4,3,2,1,0:T(8,128)(2,1)S(1)}, bf16[2,128,128]{2,1,0:T(8,128)(2,1)S(1)}, f32[2,6,8,64,128]{4,3,2,1,0:T(8,128)S(1)}) custom-call(s32[1,128]{1,0:T(1,128)} %bitcast.9, f32[128,3,128]{2,1,0:T(4,128)} %bitcast.6, f32[128,128]{1,0:T(8,128)} %bitcast.7, s32[128,128]{1,0:T(8,128)} %bitcast.8, ...), custom_call_target="tpu_custom_call" | custom-call | tf_op jit(solution)/shard_map/exchange/pallas_call | solution.py:356
  56.8 1.8 %lines.1 = f32[2,6,8,64,128]{4,3,2,1,0:T(8,128)} custom-call(bf16[2,128,128]{2,1,0:T(8,128)(2,1)S(1)} %get-tuple-element.8.matrix, bf16[16,1,2,16,256]{4,3,2,1,0:T(8,128)(2,1)S(1)} %get-tuple-element.9.part, f32[2,6,8,64,128]{4,3,2,1,0:T(8,128)S(1)} %get-tuple-element.10.done_ref), custom_call_target="tpu_custom_call" | custom-call | tf_op jit(solution)/shard_map/lines/pallas_call | solution.py:403
